TPU v7x, 256 devices: a whole 4x4x8 slice. The times are simulated.
256 devices in a mesh: row: 64 (over z, x, core), col: 4 (over y).
Axes of the slice: x: 4, y: 4, z: 8, core: 2. Of those that a mesh axis runs over, the one named last changes fastest.
Arguments:
- tiles: bfloat16 [43008, 128, 128], P(('row', 'col')), may hold values from -0.0625 to 0.0625
- tile_slots: int32 [43008], P(('row', 'col')), may hold values from 0 to 383, as said below
- sketch: bfloat16 [24576, 512], P('col'), may hold values from -6 to 6
- row_sketch: bfloat16 [65536, 512], P(('row', 'col')), may hold values from -6 to 6
- subsketch: float32 [512, 128], replicated, may hold values from -0.25 to 0.25
- couplings: bfloat16 [256, 5, 128, 128], P(('row', 'col')), may hold values from -0.25 to 0.25, as said below
Outputs:
- leaf_basis: float32 [65536, 128], P(('row', 'col'))
- transfer: float32 [256, 5, 128, 128], P(('row', 'col'))
- top_samples: float32 [256, 128, 512], P(('row', 'col'))
Inputs may be any that keep to these rules, and one draw needn't show every extreme that they name: `tile_slots`: the 168 slots of one device are distinct; slot v names row tile v // 48 and column tile v % 48. couplings[i, l] equals couplings[j, l] whenever i // 2 ** (l + 1) equals j // 2 ** (l + 1).
All inputs are finite; a program needn't handle non-finite values.
Results may differ from a plain program's by a relative error of at most 0.0003.
Values may be sent and summed in bfloat16 or wider, within the bound.
A program may use at most 128 MiB of HBM per device.

v0:
```python
import math

import jax
import jax.numpy as jnp
from jax import lax
from jax.sharding import PartitionSpec as P

LEVELS = 5


def from_partner(block, axis, bit):
    count = lax.axis_size(axis)
    route = []
    for low in range(count):
        high = low | 1 << bit
        if high != low and high < count:
            route += [(low, high), (high, low)]
    return lax.ppermute(block, axis, route)


def orthonormal(columns):
    gram = jnp.einsum("nr,nq->rq", columns, columns, precision=lax.Precision.HIGHEST)
    shift = 0.0001 * jnp.trace(gram) / gram.shape[0] + 1e-06
    lower = jnp.linalg.cholesky(gram + shift * jnp.eye(gram.shape[0], dtype=jnp.float32))
    return jax.scipy.linalg.solve_triangular(lower, columns.T, lower=True)


def leaf_step(leaf_sample, leaf_sketch, subsketch):
    reduced = jnp.dot(leaf_sample, subsketch, precision=lax.Precision.HIGHEST)
    basis_t = orthonormal(reduced)
    proj_sample = jnp.dot(basis_t, leaf_sample, precision=lax.Precision.HIGHEST)
    proj_sketch = jnp.dot(basis_t, leaf_sketch.astype(jnp.float32), precision=lax.Precision.HIGHEST)
    return (basis_t.T, proj_sample, proj_sketch)


def merge_pair(low_sample, low_sketch, high_sample, high_sketch, coupling, subsketch):
    coup_f = coupling.astype(jnp.float32)
    low_part = low_sample - jnp.dot(coup_f, high_sketch, precision=lax.Precision.HIGHEST)
    high_part = high_sample - jnp.einsum(
        "ji,js->is", coup_f, low_sketch, precision=lax.Precision.HIGHEST
    )
    stacked = jnp.concatenate([low_part, high_part], axis=0)
    stacked_sketch = jnp.concatenate([low_sketch, high_sketch], axis=0)
    reduced = jnp.dot(stacked, subsketch, precision=lax.Precision.HIGHEST)
    basis_t = orthonormal(reduced)
    new_sample = jnp.dot(basis_t, stacked, precision=lax.Precision.HIGHEST)
    new_sketch = jnp.dot(basis_t, stacked_sketch, precision=lax.Precision.HIGHEST)
    return (basis_t.T, new_sample, new_sketch)


def sample_rows(tiles, tile_slots, sketch, row_tiles):
    tile_size = tiles.shape[1]
    width = sketch.shape[1]
    col_tiles = sketch.shape[0] // tile_size
    sketch_blocks = sketch.reshape(col_tiles, tile_size, width)
    tile_count = tiles.shape[0]
    group_count = math.gcd(tile_count, 8)
    per_group = tile_count // group_count
    tile_groups = tiles.reshape(group_count, per_group, tile_size, tile_size)
    slot_groups = tile_slots.reshape(group_count, per_group)
    row_ids = jnp.arange(row_tiles, dtype=jnp.int32)

    def step(total, item):
        group_tiles, group_slots = item
        picked = jnp.take(sketch_blocks, group_slots % col_tiles, axis=0)
        product = jnp.einsum(
            "tij,tjs->tis", group_tiles, picked, preferred_element_type=jnp.float32
        )
        one_hot = (group_slots[:, None] // col_tiles == row_ids[None, :]).astype(jnp.float32)
        added = jnp.einsum("tr,tis->ris", one_hot, product, precision=lax.Precision.HIGHEST)
        return (total + added, None)

    start_total = jnp.zeros((row_tiles, tile_size, width), jnp.float32)
    total, unused = lax.scan(step, start_total, (tile_groups, slot_groups))
    return total.reshape(row_tiles * tile_size, width)


def upper_levels(proj_sample, proj_sketch, couplings, subsketch, first_level, blocks):
    rank_size = proj_sample.shape[0]
    position = lax.axis_index(("row", "col"))
    for tree_level in range(first_level, LEVELS):
        other_sample, other_sketch = from_partner(
            (proj_sample, proj_sketch), ("row", "col"), tree_level
        )
        upper = position // 2**tree_level % 2 == 1
        low_sample = jnp.where(upper, other_sample, proj_sample)
        low_sketch = jnp.where(upper, other_sketch, proj_sketch)
        high_sample = jnp.where(upper, proj_sample, other_sample)
        high_sketch = jnp.where(upper, proj_sketch, other_sketch)
        parent_basis, proj_sample, proj_sketch = merge_pair(
            low_sample, low_sketch, high_sample, high_sketch, couplings[0, tree_level], subsketch
        )
        blocks.append(jnp.where(upper, parent_basis[rank_size:], parent_basis[:rank_size]))
    return proj_sample


def per_device(tiles, tile_slots, sketch, row_sketch, subsketch, couplings):
    col_count = lax.axis_size("col")
    leaf_rows = row_sketch.shape[0]
    row_tiles = leaf_rows * col_count // tiles.shape[1]
    partial_value = sample_rows(tiles, tile_slots, sketch, row_tiles)
    blocks = []
    leaf_sample = lax.psum_scatter(partial_value, "col", scatter_dimension=0, tiled=True)
    leaf_basis, proj_sample, proj_sketch = leaf_step(leaf_sample, row_sketch, subsketch)
    top_sample = upper_levels(proj_sample, proj_sketch, couplings, subsketch, 0, blocks)
    transfer = jnp.stack(blocks, axis=0)[None]
    return (leaf_basis, transfer, top_sample[None])


def solution(mesh):
    return jax.shard_map(
        per_device,
        mesh=mesh,
        in_specs=(
            P(("row", "col"), None, None),
            P(("row", "col")),
            P("col", None),
            P(("row", "col"), None),
            P(),
            P(("row", "col"), None, None, None),
        ),
        out_specs=(
            P(("row", "col"), None),
            P(("row", "col"), None, None, None),
            P(("row", "col"), None, None),
        ),
        check_vma=False,
    )
```

profile of v0, /device:TPU:192, one launch (start us, length us, event | category | flops | bytes accessed | tf_op | source)
XLA Modules:
  0.0 414.4 jit_solution(16988987369060565091)
XLA Ops:
  8.0 140.1 %while.13 = (s32[]{:T(128)}, f32[8,128,512]{2,0,1:T(8,128)}, s32[8,21]{1,0:T(8,128)S(1)}, bf16[8,21,128,128]{3,2,1,0:T(8,128)(2,1)}, bf16[48,128,512]{2,1,0:T(8,128)(2,1)}, /*index=5*/s32[]{:T(128)}, s32[]{:T(128)}) while((s32[]{:T(128)}, f32[8,128,512]{2,0,1:T(8,128)}, s32[8,21]{1,0:T(8,128)S(1)}, ...), condition=%wide.region_1.2_spmd.clone, body=%wide.region_0.1_spmd.clone.sunk | while | flops 486868736 | bytes 24154936 | solution.py:74
  8.1 3.5 gather_fusion
  11.6 4.4 %fusion.197 = f32[21,128,512]{2,1,0:T(8,128)} fusion(bf16[21,128,512]{2,1,0:T(8,128)(2,1)S(1)} %gather_fusion, pred[21]{0:T(512)(128)(4,1)S(1)} %compare_and_fusion.2, bf16[8,21,128,128]{3,2,1,0:T(8,128)(2,1)} %get-tuple-element.190, s32[]{:T(128)S(6)} %copy.65), kind=kOutput, calls=%fused_computation.4.clone.1 | convolution fusion | flops 353697792 | bytes 8945689 | tf_op jit(solution)/shard_map/while/body/eval_jaxpr/tij,tjs->tis/dot_general | solution.py:66
  16.0 8.9 %select_add_fusion.8 = f32[8,128,512]{2,0,1:T(8,128)} fusion(f32[8,128,512]{2,0,1:T(8,128)} %get-tuple-element.181, f32[21,128,512]{2,1,0:T(8,128)} %fusion.197, pred[]{:T(512)S(6)} %compare.25, s32[21]{0:T(128)S(1)} %fusion.198), kind=kOutput, calls=%fused_computation.7.clone.1 | convolution fusion | flops 133169320 | bytes 9699413 | tf_op jit(solution)/shard_map/while/body/eval_jaxpr/tr,tis->ris/dot_general | solution.py:70
  25.0 3.5 gather_fusion
  28.5 4.4 %fusion.197 = f32[21,128,512]{2,1,0:T(8,128)} fusion(bf16[21,128,512]{2,1,0:T(8,128)(2,1)S(1)} %gather_fusion, pred[21]{0:T(512)(128)(4,1)S(1)} %compare_and_fusion.2, bf16[8,21,128,128]{3,2,1,0:T(8,128)(2,1)} %get-tuple-element.190, s32[]{:T(128)S(6)} %copy.65), kind=kOutput, calls=%fused_computation.4.clone.1 | convolution fusion | flops 353697792 | bytes 8945689 | tf_op jit(solution)/shard_map/while/body/eval_jaxpr/tij,tjs->tis/dot_general | solution.py:66
  32.9 9.5 %select_add_fusion.8 = f32[8,128,512]{2,0,1:T(8,128)} fusion(f32[8,128,512]{2,0,1:T(8,128)} %get-tuple-element.181, f32[21,128,512]{2,1,0:T(8,128)} %fusion.197, pred[]{:T(512)S(6)} %compare.25, s32[21]{0:T(128)S(1)} %fusion.198), kind=kOutput, calls=%fused_computation.7.clone.1 | convolution fusion | flops 133169320 | bytes 9699413 | tf_op jit(solution)/shard_map/while/body/eval_jaxpr/tr,tis->ris/dot_general | solution.py:70
  42.5 3.5 gather_fusion
  46.1 4.4 %fusion.197 = f32[21,128,512]{2,1,0:T(8,128)} fusion(bf16[21,128,512]{2,1,0:T(8,128)(2,1)S(1)} %gather_fusion, pred[21]{0:T(512)(128)(4,1)S(1)} %compare_and_fusion.2, bf16[8,21,128,128]{3,2,1,0:T(8,128)(2,1)} %get-tuple-element.190, s32[]{:T(128)S(6)} %copy.65), kind=kOutput, calls=%fused_computation.4.clone.1 | convolution fusion | flops 353697792 | bytes 8945689 | tf_op jit(solution)/shard_map/while/body/eval_jaxpr/tij,tjs->tis/dot_general | solution.py:66
  50.5 9.5 %select_add_fusion.8 = f32[8,128,512]{2,0,1:T(8,128)} fusion(f32[8,128,512]{2,0,1:T(8,128)} %get-tuple-element.181, f32[21,128,512]{2,1,0:T(8,128)} %fusion.197, pred[]{:T(512)S(6)} %compare.25, s32[21]{0:T(128)S(1)} %fusion.198), kind=kOutput, calls=%fused_computation.7.clone.1 | convolution fusion | flops 133169320 | bytes 9699413 | tf_op jit(solution)/shard_map/while/body/eval_jaxpr/tr,tis->ris/dot_general | solution.py:70
  60.1 3.5 gather_fusion
  63.6 4.4 %fusion.197 = f32[21,128,512]{2,1,0:T(8,128)} fusion(bf16[21,128,512]{2,1,0:T(8,128)(2,1)S(1)} %gather_fusion, pred[21]{0:T(512)(128)(4,1)S(1)} %compare_and_fusion.2, bf16[8,21,128,128]{3,2,1,0:T(8,128)(2,1)} %get-tuple-element.190, s32[]{:T(128)S(6)} %copy.65), kind=kOutput, calls=%fused_computation.4.clone.1 | convolution fusion | flops 353697792 | bytes 8945689 | tf_op jit(solution)/shard_map/while/body/eval_jaxpr/tij,tjs->tis/dot_general | solution.py:66
  68.1 9.5 %select_add_fusion.8 = f32[8,128,512]{2,0,1:T(8,128)} fusion(f32[8,128,512]{2,0,1:T(8,128)} %get-tuple-element.181, f32[21,128,512]{2,1,0:T(8,128)} %fusion.197, pred[]{:T(512)S(6)} %compare.25, s32[21]{0:T(128)S(1)} %fusion.198), kind=kOutput, calls=%fused_computation.7.clone.1 | convolution fusion | flops 133169320 | bytes 9699413 | tf_op jit(solution)/shard_map/while/body/eval_jaxpr/tr,tis->ris/dot_general | solution.py:70
  77.6 3.5 gather_fusion
  81.2 4.4 %fusion.197 = f32[21,128,512]{2,1,0:T(8,128)} fusion(bf16[21,128,512]{2,1,0:T(8,128)(2,1)S(1)} %gather_fusion, pred[21]{0:T(512)(128)(4,1)S(1)} %compare_and_fusion.2, bf16[8,21,128,128]{3,2,1,0:T(8,128)(2,1)} %get-tuple-element.190, s32[]{:T(128)S(6)} %copy.65), kind=kOutput, calls=%fused_computation.4.clone.1 | convolution fusion | flops 353697792 | bytes 8945689 | tf_op jit(solution)/shard_map/while/body/eval_jaxpr/tij,tjs->tis/dot_general | solution.py:66
  85.6 9.5 %select_add_fusion.8 = f32[8,128,512]{2,0,1:T(8,128)} fusion(f32[8,128,512]{2,0,1:T(8,128)} %get-tuple-element.181, f32[21,128,512]{2,1,0:T(8,128)} %fusion.197, pred[]{:T(512)S(6)} %compare.25, s32[21]{0:T(128)S(1)} %fusion.198), kind=kOutput, calls=%fused_computation.7.clone.1 | convolution fusion | flops 133169320 | bytes 9699413 | tf_op jit(solution)/shard_map/while/body/eval_jaxpr/tr,tis->ris/dot_general | solution.py:70
  95.2 3.5 gather_fusion
  98.7 4.4 %fusion.197 = f32[21,128,512]{2,1,0:T(8,128)} fusion(bf16[21,128,512]{2,1,0:T(8,128)(2,1)S(1)} %gather_fusion, pred[21]{0:T(512)(128)(4,1)S(1)} %compare_and_fusion.2, bf16[8,21,128,128]{3,2,1,0:T(8,128)(2,1)} %get-tuple-element.190, s32[]{:T(128)S(6)} %copy.65), kind=kOutput, calls=%fused_computation.4.clone.1 | convolution fusion | flops 353697792 | bytes 8945689 | tf_op jit(solution)/shard_map/while/body/eval_jaxpr/tij,tjs->tis/dot_general | solution.py:66
  103.2 9.5 %select_add_fusion.8 = f32[8,128,512]{2,0,1:T(8,128)} fusion(f32[8,128,512]{2,0,1:T(8,128)} %get-tuple-element.181, f32[21,128,512]{2,1,0:T(8,128)} %fusion.197, pred[]{:T(512)S(6)} %compare.25, s32[21]{0:T(128)S(1)} %fusion.198), kind=kOutput, calls=%fused_computation.7.clone.1 | convolution fusion | flops 133169320 | bytes 9699413 | tf_op jit(solution)/shard_map/while/body/eval_jaxpr/tr,tis->ris/dot_general | solution.py:70
  112.7 3.5 gather_fusion
  116.3 4.4 %fusion.197 = f32[21,128,512]{2,1,0:T(8,128)} fusion(bf16[21,128,512]{2,1,0:T(8,128)(2,1)S(1)} %gather_fusion, pred[21]{0:T(512)(128)(4,1)S(1)} %compare_and_fusion.2, bf16[8,21,128,128]{3,2,1,0:T(8,128)(2,1)} %get-tuple-element.190, s32[]{:T(128)S(6)} %copy.65), kind=kOutput, calls=%fused_computation.4.clone.1 | convolution fusion | flops 353697792 | bytes 8945689 | tf_op jit(solution)/shard_map/while/body/eval_jaxpr/tij,tjs->tis/dot_general | solution.py:66
  120.7 9.5 %select_add_fusion.8 = f32[8,128,512]{2,0,1:T(8,128)} fusion(f32[8,128,512]{2,0,1:T(8,128)} %get-tuple-element.181, f32[21,128,512]{2,1,0:T(8,128)} %fusion.197, pred[]{:T(512)S(6)} %compare.25, s32[21]{0:T(128)S(1)} %fusion.198), kind=kOutput, calls=%fused_computation.7.clone.1 | convolution fusion | flops 133169320 | bytes 9699413 | tf_op jit(solution)/shard_map/while/body/eval_jaxpr/tr,tis->ris/dot_general | solution.py:70
  130.3 3.5 gather_fusion
  133.8 4.4 %fusion.197 = f32[21,128,512]{2,1,0:T(8,128)} fusion(bf16[21,128,512]{2,1,0:T(8,128)(2,1)S(1)} %gather_fusion, pred[21]{0:T(512)(128)(4,1)S(1)} %compare_and_fusion.2, bf16[8,21,128,128]{3,2,1,0:T(8,128)(2,1)} %get-tuple-element.190, s32[]{:T(128)S(6)} %copy.65), kind=kOutput, calls=%fused_computation.4.clone.1 | convolution fusion | flops 353697792 | bytes 8945689 | tf_op jit(solution)/shard_map/while/body/eval_jaxpr/tij,tjs->tis/dot_general | solution.py:66
  138.3 9.5 %select_add_fusion.8 = f32[8,128,512]{2,0,1:T(8,128)} fusion(f32[8,128,512]{2,0,1:T(8,128)} %get-tuple-element.181, f32[21,128,512]{2,1,0:T(8,128)} %fusion.197, pred[]{:T(512)S(6)} %compare.25, s32[21]{0:T(128)S(1)} %fusion.198), kind=kOutput, calls=%fused_computation.7.clone.1 | convolution fusion | flops 133169320 | bytes 9699413 | tf_op jit(solution)/shard_map/while/body/eval_jaxpr/tr,tis->ris/dot_general | solution.py:70
  148.1 4.2 %copy.29 = f32[8,128,512]{2,1,0:T(8,128)} copy(f32[8,128,512]{2,0,1:T(8,128)} %get-tuple-element.85) | data formatting | bytes 4194304 | tf_op jit(solution)/shard_map/while | solution.py:74
  152.3 33.2 %reduce-scatter.2.cloned.1.call-done = f32[256,512]{1,0:T(8,128)} async-done(((f32[1024,512]{1,0:T(8,128)}), f32[256,512]{1,0:T(8,128)}) %reduce-scatter.2.cloned.1.call-update) | async-done | bytes 524304 | tf_op jit(solution)/shard_map/reduce_scatter | solution.py:103
  189.0 11.7 %cholesky.104 = f32[128,128]{1,0:T(8,128)S(1)} custom-call(f32[128,128]{1,0:T(8,128)S(1)} %fusion.91), custom_call_target="Cholesky" | custom-call | tf_op jit(solution)/shard_map/jit(cholesky)/cholesky | solution.py:24
  202.1 9.8 %custom-call.11 = f32[1,128,128]{1,2,0:T(8,128)S(1)} custom-call(f32[1,128,128]{2,1,0:T(8,128)S(1)} %fusion.64), custom_call_target="InvertDiagBlocksLowerTriangular" | custom-call | tf_op jit(solution)/shard_map/jit(_solve_triangular)/triangular_solve | solution.py:25
  215.6 6.1 %collective-permute-done.1 = f32[128,512]{1,0:T(8,128)S(1)} collective-permute-done((f32[128,512]{1,0:T(8,128)S(1)}, f32[128,512]{1,0:T(8,128)S(1)}, u32[]{:S(2)}, u32[]{:S(2)}) %collective-permute-start.1) | collective-permute-done | bytes 262176 | tf_op jit(solution)/shard_map/ppermute | solution.py:18
  221.8 4.4 %collective-permute-done = f32[128,512]{1,0:T(8,128)S(1)} collective-permute-done((f32[128,512]{1,0:T(8,128)S(1)}, f32[128,512]{1,0:T(8,128)S(1)}, u32[]{:S(2)}, u32[]{:S(2)}) %collective-permute-start) | collective-permute-done | bytes 262176 | tf_op jit(solution)/shard_map/ppermute | solution.py:18
  229.2 11.7 %cholesky.115 = f32[128,128]{1,0:T(8,128)S(1)} custom-call(f32[128,128]{1,0:T(8,128)S(1)} %fusion.89), custom_call_target="Cholesky" | custom-call | tf_op jit(solution)/shard_map/jit(cholesky)/cholesky | solution.py:24
  242.2 9.8 %custom-call.12 = f32[1,128,128]{1,2,0:T(8,128)S(1)} custom-call(f32[1,128,128]{2,1,0:T(8,128)S(1)} %fusion.65), custom_call_target="InvertDiagBlocksLowerTriangular" | custom-call | tf_op jit(solution)/shard_map/jit(_solve_triangular)/triangular_solve | solution.py:25
  257.9 5.7 %collective-permute-done.3 = f32[128,512]{1,0:T(8,128)S(1)} collective-permute-done((f32[128,512]{1,0:T(8,128)S(1)}, f32[128,512]{1,0:T(8,128)S(1)}, u32[]{:S(2)}, u32[]{:S(2)}) %collective-permute-start.3) | collective-permute-done | bytes 262176 | tf_op jit(solution)/shard_map/ppermute | solution.py:18
  263.6 3.5 collective-permute-done.2
  270.2 11.7 %cholesky.126 = f32[128,128]{1,0:T(8,128)S(1)} custom-call(f32[128,128]{1,0:T(8,128)S(1)} %fusion.87), custom_call_target="Cholesky" | custom-call | tf_op jit(solution)/shard_map/jit(cholesky)/cholesky | solution.py:24
  283.2 9.8 %custom-call.13 = f32[1,128,128]{1,2,0:T(8,128)S(1)} custom-call(f32[1,128,128]{2,1,0:T(8,128)S(1)} %fusion.66), custom_call_target="InvertDiagBlocksLowerTriangular" | custom-call | tf_op jit(solution)/shard_map/jit(_solve_triangular)/triangular_solve | solution.py:25
  299.3 11.7 %cholesky.137 = f32[128,128]{1,0:T(8,128)S(1)} custom-call(f32[128,128]{1,0:T(8,128)S(1)} %fusion.85), custom_call_target="Cholesky" | custom-call | tf_op jit(solution)/shard_map/jit(cholesky)/cholesky | solution.py:24
  312.3 9.8 %custom-call.14 = f32[1,128,128]{1,2,0:T(8,128)S(1)} custom-call(f32[1,128,128]{2,1,0:T(8,128)S(1)} %fusion.67), custom_call_target="InvertDiagBlocksLowerTriangular" | custom-call | tf_op jit(solution)/shard_map/jit(_solve_triangular)/triangular_solve | solution.py:25
  325.9 6.2 %collective-permute-done.7 = f32[128,512]{1,0:T(8,128)S(1)} collective-permute-done((f32[128,512]{1,0:T(8,128)S(1)}, f32[128,512]{1,0:T(8,128)S(1)}, u32[]{:S(2)}, u32[]{:S(2)}) %collective-permute-start.7) | collective-permute-done | bytes 262176 | tf_op jit(solution)/shard_map/ppermute | solution.py:18
  332.2 5.0 %collective-permute-done.6 = f32[128,512]{1,0:T(8,128)S(1)} collective-permute-done((f32[128,512]{1,0:T(8,128)S(1)}, f32[128,512]{1,0:T(8,128)S(1)}, u32[]{:S(2)}, u32[]{:S(2)}) %collective-permute-start.6) | collective-permute-done | bytes 262176 | tf_op jit(solution)/shard_map/ppermute | solution.py:18
  340.2 11.7 %cholesky.148 = f32[128,128]{1,0:T(8,128)S(1)} custom-call(f32[128,128]{1,0:T(8,128)S(1)} %fusion.83), custom_call_target="Cholesky" | custom-call | tf_op jit(solution)/shard_map/jit(cholesky)/cholesky | solution.py:24
  353.2 9.8 %custom-call.15 = f32[1,128,128]{1,2,0:T(8,128)S(1)} custom-call(f32[1,128,128]{2,1,0:T(8,128)S(1)} %fusion.68), custom_call_target="InvertDiagBlocksLowerTriangular" | custom-call | tf_op jit(solution)/shard_map/jit(_solve_triangular)/triangular_solve | solution.py:25
  364.2 3.1 collective-permute-start.8
  368.0 7.0 %collective-permute-done.8 = f32[128,512]{1,0:T(8,128)S(1)} collective-permute-done((f32[128,512]{1,0:T(8,128)S(1)}, f32[128,512]{1,0:T(8,128)S(1)}, u32[]{:S(2)}, u32[]{:S(2)}) %collective-permute-start.8) | collective-permute-done | bytes 262176 | tf_op jit(solution)/shard_map/ppermute | solution.py:18
  375.0 4.2 %collective-permute-done.9 = f32[128,512]{1,0:T(8,128)S(1)} collective-permute-done((f32[128,512]{1,0:T(8,128)S(1)}, f32[128,512]{1,0:T(8,128)S(1)}, u32[]{:S(2)}, u32[]{:S(2)}) %collective-permute-start.9) | collective-permute-done | bytes 262176 | tf_op jit(solution)/shard_map/ppermute | solution.py:18
  382.2 11.7 %cholesky.159 = f32[128,128]{1,0:T(8,128)S(1)} custom-call(f32[128,128]{1,0:T(8,128)S(1)} %fusion.81), custom_call_target="Cholesky" | custom-call | tf_op jit(solution)/shard_map/jit(cholesky)/cholesky | solution.py:24
  395.2 9.8 %custom-call.16 = f32[1,128,128]{1,2,0:T(8,128)S(1)} custom-call(f32[1,128,128]{2,1,0:T(8,128)S(1)} %fusion.69), custom_call_target="InvertDiagBlocksLowerTriangular" | custom-call | tf_op jit(solution)/shard_map/jit(_solve_triangular)/triangular_solve | solution.py:25
  (141 shorter events, 44.5 us)
Async XLA Ops:
  7.2 178.4 %copy-start = (f32[512,128]{1,0:T(8,128)S(1)}, f32[512,128]{1,0:T(8,128)}, u32[]{:S(2)}) copy-start(f32[512,128]{1,0:T(8,128)} %param.15) | copy-start | bytes 786436
  7.2 178.3 %reduce-scatter.2.cloned.1.call-start = ((), (), s32[]{:S(2)}) async-start(), calls=%async_computation.1 | async-start | bytes 2621440 | tf_op jit(solution)/shard_map/reduce_scatter | solution.py:103
  152.3 59.9 %copy-start.3 = (bf16[256,512]{1,0:T(8,128)(2,1)S(1)}, bf16[256,512]{1,0:T(8,128)(2,1)}, u32[]{:S(2)}) copy-start(bf16[256,512]{1,0:T(8,128)(2,1)} %param.14) | copy-start | bytes 786436
  152.3 73.9 %copy-start.2 = (bf16[1,5,128,128]{3,2,1,0:T(8,128)(2,1)S(1)}, bf16[1,5,128,128]{3,2,1,0:T(8,128)(2,1)}, u32[]{:S(2)}) copy-start(bf16[1,5,128,128]{3,2,1,0:T(8,128)(2,1)} %param.16) | copy-start | bytes 491524
  185.5 27.3 %copy-start.1 = (f32[256,512]{1,0:T(8,128)S(1)}, f32[256,512]{1,0:T(8,128)}, u32[]{:S(2)}) copy-start(f32[256,512]{1,0:T(8,128)} %reduce-scatter.2.cloned.1.call-done) | copy-start | bytes 1572868
  212.5 9.3 %collective-permute-start.1 = (f32[128,512]{1,0:T(8,128)S(1)}, f32[128,512]{1,0:T(8,128)S(1)}, u32[]{:S(2)}, u32[]{:S(2)}) collective-permute-start(f32[128,512]{1,0:T(8,128)S(1)} %fusion.144), channel_id=1, source_target_pairs={{0,1},{1,0},{2,3},{3,2},{4,5},{5,4},{6,7},{7,6},{8,9},{9,8},{10,11... | collective-permute-start | bytes 786440 | tf_op jit(solution)/shard_map/ppermute | solution.py:18
  213.3 12.9 %collective-permute-start = (f32[128,512]{1,0:T(8,128)S(1)}, f32[128,512]{1,0:T(8,128)S(1)}, u32[]{:S(2)}, u32[]{:S(2)}) collective-permute-start(f32[128,512]{1,0:T(8,128)S(1)} %fusion.143), channel_id=1, source_target_pairs={{0,1},{1,0},{2,3},{3,2},{4,5},{5,4},{6,7},{7,6},{8,9},{9,8},{10,11... | collective-permute-start | bytes 786440 | tf_op jit(solution)/shard_map/ppermute | solution.py:18
  252.8 10.8 %collective-permute-start.3 = (f32[128,512]{1,0:T(8,128)S(1)}, f32[128,512]{1,0:T(8,128)S(1)}, u32[]{:S(2)}, u32[]{:S(2)}) collective-permute-start(f32[128,512]{1,0:T(8,128)S(1)} %fusion.19), channel_id=1, source_target_pairs={{0,2},{2,0},{1,3},{3,1},{4,6},{6,4},{5,7},{7,5},{8,10},{10,8},{9,1... | collective-permute-start | bytes 786440 | tf_op jit(solution)/shard_map/ppermute | solution.py:18
  254.8 12.4 %collective-permute-start.2 = (f32[128,512]{1,0:T(8,128)S(1)}, f32[128,512]{1,0:T(8,128)S(1)}, u32[]{:S(2)}, u32[]{:S(2)}) collective-permute-start(f32[128,512]{1,0:T(8,128)S(1)} %fusion.42), channel_id=1, source_target_pairs={{0,2},{2,0},{1,3},{3,1},{4,6},{6,4},{5,7},{7,5},{8,10},{10,8},{9,1... | collective-permute-start | bytes 786440 | tf_op jit(solution)/shard_map/ppermute | solution.py:18
  293.8 1.6 collective-permute-start.5
  294.3 2.0 collective-permute-start.4
  322.9 9.3 %collective-permute-start.7 = (f32[128,512]{1,0:T(8,128)S(1)}, f32[128,512]{1,0:T(8,128)S(1)}, u32[]{:S(2)}, u32[]{:S(2)}) collective-permute-start(f32[128,512]{1,0:T(8,128)S(1)} %fusion.27), channel_id=1, source_target_pairs={{0,8},{8,0},{1,9},{9,1},{2,10},{10,2},{3,11},{11,3},{4,12},{12,4},... | collective-permute-start | bytes 786440 | tf_op jit(solution)/shard_map/ppermute | solution.py:18
  324.8 12.3 %collective-permute-start.6 = (f32[128,512]{1,0:T(8,128)S(1)}, f32[128,512]{1,0:T(8,128)S(1)}, u32[]{:S(2)}, u32[]{:S(2)}) collective-permute-start(f32[128,512]{1,0:T(8,128)S(1)} %fusion.38), channel_id=1, source_target_pairs={{0,8},{8,0},{1,9},{9,1},{2,10},{10,2},{3,11},{11,3},{4,12},{12,4},... | collective-permute-start | bytes 786440 | tf_op jit(solution)/shard_map/ppermute | solution.py:18
  364.2 10.8 %collective-permute-start.8 = (f32[128,512]{1,0:T(8,128)S(1)}, f32[128,512]{1,0:T(8,128)S(1)}, u32[]{:S(2)}, u32[]{:S(2)}) collective-permute-start(f32[128,512]{1,0:T(8,128)S(1)} %fusion.36), channel_id=1, source_target_pairs={{0,16},{16,0},{1,17},{17,1},{2,18},{18,2},{3,19},{19,3},{4,20},{20... | collective-permute-start | bytes 786440 | tf_op jit(solution)/shard_map/ppermute | solution.py:18
  367.3 11.9 %collective-permute-start.9 = (f32[128,512]{1,0:T(8,128)S(1)}, f32[128,512]{1,0:T(8,128)S(1)}, u32[]{:S(2)}, u32[]{:S(2)}) collective-permute-start(f32[128,512]{1,0:T(8,128)S(1)} %fusion.31), channel_id=1, source_target_pairs={{0,16},{16,0},{1,17},{17,1},{2,18},{18,2},{3,19},{19,3},{4,20},{20... | collective-permute-start | bytes 786440 | tf_op jit(solution)/shard_map/ppermute | solution.py:18
Sparse Core Ops, SparseCore 0:
  152.4 33.0 reduce-scatter.1
where the time goes:
time: 423 us; the launch traced here: 414 us
  other arithmetic  138 us (33%)
  matrix products  132 us (31%)
  waiting for transfers between devices  76.4 us (18%)
  local copies, waits for them, and re-layouts  35.2 us (8%)
  between operations  18.7 us (4%)
  starting transfers between devices  13.9 us (3%)
    dot_general x8, matrix products, step(): jnp.einsum('tr,tis->ris', one_hot, product, precision=lax.Precision.HIGHEST)  75.7 us
    another operation x18, other arithmetic, orthonormal(): jnp.linalg.cholesky(gram + shift * jnp.eye(gram.shape[0], dtype=jnp.float...  74.3 us
    another operation x12, other arithmetic, orthonormal(): return jax.scipy.linalg.solve_triangular(lower, columns.T, lower=True)  62.8 us
    ppermute x10, waiting for transfers between devices, from_partner(): return lax.ppermute(block, axis, route)  43.2 us
    dot_general x8, matrix products, step(): jnp.einsum('tij,tjs->tis', group_tiles, picked, preferred_element_type=jn...  35.4 us
    reduce_scatter x1, waiting for transfers between devices, per_device(): lax.psum_scatter(partial_value, 'col', scatter_dimension=0, tiled=True)  33.2 us
    gather x8, local copies, waits for them, and re-layouts, step(): picked = jnp.take(sketch_blocks, group_slots % col_tiles, axis=0)  28.1 us
    ppermute x10, starting transfers between devices, from_partner(): return lax.ppermute(block, axis, route)  13.9 us
  transfers between devices with their start and end apart: 11, of which 11 were waited for; matrix products, arithmetic and copies ran while one was open for 1% of the time, Pallas kernels for 0%

commit v1 on v0

v1 whole, which is shorter than its diff:
```python
import functools

import jax
import jax.numpy as jnp
from jax import lax
from jax.experimental import pallas as pl
from jax.experimental.pallas import tpu as pltpu
from jax.sharding import PartitionSpec as P

LEVELS = 5
R = 128
F32 = jnp.float32
BF = jnp.bfloat16
HI = lax.Precision.HIGHEST
MESH = pl.DeviceIdType.MESH
LOW, HIGH = pl.ds(0, R), pl.ds(R, R)


def dot(a, b, ca=1, cb=0):
    return lax.dot_general(a, b, (((ca,), (cb,)), ((), ())), precision=HI, preferred_element_type=F32)


def dot16(a, b, ca=1, cb=0):
    return lax.dot_general(a, b, (((ca,), (cb,)), ((), ())), preferred_element_type=F32)


def split3(x):
    hi = x.astype(BF)
    rest = x - hi.astype(F32)
    mid = rest.astype(BF)
    return hi, mid, (rest - mid.astype(F32)).astype(BF)


def dot_bx(b, x, ca=1, cb=0):
    hi, mid, low = split3(x)
    return dot16(b, hi, ca, cb) + (dot16(b, mid, ca, cb) + dot16(b, low, ca, cb))


def dot_xb(x, b, ca=1, cb=0):
    hi, mid, low = split3(x)
    return dot16(hi, b, ca, cb) + (dot16(mid, b, ca, cb) + dot16(low, b, ca, cb))


def sample_kernel(step, slots_ref, tiles_ref, sketch_ref, sub_ref, y_ref, z_ref, dense, sk, present, tsem, ssem):
    tile_count = tiles_ref.shape[0]
    col_tiles = dense.shape[0]
    row_tiles = dense.shape[1] // R
    sketch_copy = pltpu.make_async_copy(sketch_ref, sk, ssem)
    sketch_copy.start()

    @pl.loop(0, present.shape[0], unroll=8)
    def _(v):
        present[v] = 0

    @pl.loop(0, tile_count, unroll=4)
    def _(t):
        v = slots_ref[t]
        present[v] = 1
        r = v // col_tiles
        rows = pl.ds(pl.multiple_of(r * R, R), R)
        pltpu.make_async_copy(tiles_ref.at[t], dense.at[v - r * col_tiles, rows, :], tsem).start()

    zero = jnp.zeros((R, R), BF)

    @pl.loop(0, present.shape[0])
    def _(v):
        @pl.when(present[v] == 0)
        def _():
            r = v // col_tiles
            dense[v - r * col_tiles, pl.ds(pl.multiple_of(r * R, R), R), :] = zero

    sketch_copy.wait()
    arrived = dense.at[pl.ds(0, tile_count // row_tiles)]
    pltpu.make_async_copy(arrived, arrived, tsem).wait()
    y_ref[...] = jnp.zeros_like(y_ref)

    @pl.loop(0, col_tiles // step)
    def _(p):
        lhs = jnp.concatenate([dense[p * step + i] for i in range(step)], axis=1)
        rhs = sk[pl.ds(pl.multiple_of(p * step * R, R), step * R), :]
        y_ref[...] += jnp.dot(lhs, rhs, preferred_element_type=F32)

    z_ref[...] = dot(y_ref[...], sub_ref[...])


def run_sample(tiles, slots, sketch, subsketch, row_tiles):
    col_tiles = sketch.shape[0] // R
    rows, width = row_tiles * R, sketch.shape[1]
    vmem = pl.BlockSpec(memory_space=pltpu.VMEM)
    hbm = pl.BlockSpec(memory_space=pl.ANY)
    return pl.pallas_call(
        functools.partial(sample_kernel, 8),
        out_shape=[jax.ShapeDtypeStruct((rows, width), F32), jax.ShapeDtypeStruct((rows, R), F32)],
        in_specs=[pl.BlockSpec(memory_space=pltpu.SMEM), hbm, hbm, vmem],
        out_specs=[vmem, vmem],
        scratch_shapes=[
            pltpu.VMEM((col_tiles, rows, R), BF),
            pltpu.VMEM(sketch.shape, BF),
            pltpu.SMEM((row_tiles * col_tiles,), jnp.int32),
            pltpu.SemaphoreType.DMA,
            pltpu.SemaphoreType.DMA,
        ],
        compiler_params=pltpu.CompilerParams(vmem_limit_bytes=60 * 2**20),
        name="sample",
    )(slots, tiles, sketch, subsketch)


def row_of(x, k):
    return jnp.broadcast_to(x[k : k + 1, :], x.shape)


def factor(ax, lt, middle):
    blocks = ax.shape[0]
    sub = lax.broadcasted_iota(jnp.int32, (8, 2 * R), 0)
    for j in range(blocks):
        if j == blocks // 2:
            middle()
        own = ax[j]
        cols = [jnp.broadcast_to(own[:, 8 * j + k : 8 * j + k + 1], (8, R)) for k in range(8)]
        d = [[row_of(cols[k], i) if i >= k else None for k in range(8)] for i in range(8)]
        rows = [row_of(own, k) for k in range(8)]
        inv, mult = [], [[None] * 8 for _ in range(8)]
        for k in range(8):
            inv.append(1.0 / d[k][k])
            for i in range(k + 1, 8):
                m = d[i][k] * inv[k]
                mult[i][k] = jnp.concatenate([m, m], axis=1)
                for i2 in range(i, 8):
                    d[i2][i] = d[i2][i] - d[i2][k] * m
                rows[i] = rows[i] - mult[i][k] * rows[k]
        out = rows[0]
        pivots = d[0][0]
        for k in range(1, 8):
            out = jnp.where(sub == k, rows[k], out)
            pivots = jnp.where(sub[:, :R] == k, d[k][k], pivots)
        scale = lax.rsqrt(pivots)
        lt[pl.ds(8 * j, 8), :] = out[:, :R] * scale
        ax[j, :, pl.ds(R, R)] = out[:, R:] * scale
        if j == blocks - 1:
            break
        q = [rows[k] * jnp.concatenate([inv[k], inv[k]], axis=1) for k in range(8)]
        for k in range(7, 0, -1):
            for i in range(k):
                q[i] = q[i] - mult[k][i] * q[k]
        for g in range(j + 1, blocks):
            rest = ax[g]
            terms = []
            for k in range(8):
                c = jnp.broadcast_to(rest[:, 8 * j + k : 8 * j + k + 1], (8, 2 * R))
                terms.append(c * q[k])
            while len(terms) > 1:
                terms = [terms[i] + terms[i + 1] for i in range(0, len(terms), 2)]
            ax[g] = rest - terms[0]


def tree_kernel(
    zpart, ypart, wrow, subsk, coup,
    leaf_out, trans_out, top_out,
    ax, lt, zb, wst, ub, comm, comm2, relay, fin, staged, sparts, vbuf, topbuf, cbuf, ybuf, ps,
    rs_send, rs_recv, ag_send, ag_recv, c_send, c_recv, c2_send, c2_recv, ysem,
):
    row, col = lax.axis_index("row"), lax.axis_index("col")
    position = row * 4 + col
    right, left = (col + 1) % 4, (col + 3) % 4
    across = (col + 2) % 4
    to_right, to_left = (row, right), (row, left)
    chip = row // 2
    core = row - chip * 2
    plane = chip // 4
    x = chip - plane * 4
    x_near = x + 1 - 2 * (x % 2)
    partners = [
        (row, col + 1 - 2 * (col % 2)),
        (row, 3 - col),
        (row + 1 - 2 * core, col),
        ((plane * 4 + x_near) * 2 + core, col),
        ((plane * 4 + 3 - x) * 2 + core, col),
    ]
    upper = [(position // 2**t) % 2 for t in range(LEVELS)]

    barrier = pltpu.get_barrier_semaphore()
    peers = [to_right, to_left] + partners[2:]
    for peer in peers:
        pl.semaphore_signal(barrier, inc=1, device_id=peer, device_id_type=MESH)
    pl.semaphore_wait(barrier, len(peers))

    def remote(src, dst, send, recv, peer):
        return pltpu.make_async_remote_copy(
            src_ref=src, dst_ref=dst, send_sem=send, recv_sem=recv, device_id=peer, device_id_type=MESH
        )

    def rs_copy(parts, n, i):
        src, dst, peer = [
            (parts.at[across, LOW], relay.at[n, 0], to_right),
            (parts.at[across, HIGH], relay.at[n, 1], to_left),
            (parts.at[right, HIGH], fin.at[n, 1], to_right),
            (parts.at[left, LOW], fin.at[n, 2], to_left),
            (staged.at[n, 0], fin.at[n, 0], to_right),
            (staged.at[n, 1], fin.at[n, 3], to_left),
        ][i]
        return remote(src, dst, rs_send.at[n, i], rs_recv.at[n, i], peer)

    def rs_first(parts, n):
        for i in range(4):
            rs_copy(parts, n, i).start()

    def rs_second(parts, n):
        rs_copy(parts, n, 0).wait_recv()
        staged[n, 0] = parts[right, LOW] + relay[n, 0]
        rs_copy(parts, n, 4).start()
        rs_copy(parts, n, 1).wait_recv()
        staged[n, 1] = parts[left, HIGH] + relay[n, 1]
        rs_copy(parts, n, 5).start()

    def rs_last(parts, n, out):
        for i in range(2, 6):
            rs_copy(parts, n, i).wait_recv()
        out[LOW] = parts[col, LOW] + (fin[n, 0] + fin[n, 2])
        out[HIGH] = parts[col, HIGH] + (fin[n, 1] + fin[n, 3])

    def rs_drain(parts, n):
        for i in range(6):
            rs_copy(parts, n, i).wait_send()

    def ag_copy(buf, n, i, receive=False):
        half = buf.shape[1] // 2
        first, second = pl.ds(0, half), pl.ds(half, half)
        if receive:
            ref = [buf.at[left], buf.at[right], buf.at[across, first], buf.at[across, second]][i]
        else:
            ref = [buf.at[col], buf.at[col], buf.at[left, first], buf.at[right, second]][i]
        return remote(ref, ref, ag_send.at[n, i], ag_recv.at[n, i], [to_right, to_left][i % 2])

    def ag_first(buf, n):
        for i in range(2):
            ag_copy(buf, n, i).start()

    def ag_second(buf, n):
        for i in range(2):
            ag_copy(buf, n, i, True).wait_recv()
            ag_copy(buf, n, i + 2).start()

    def ag_last(buf, n):
        for i in range(2, 4):
            ag_copy(buf, n, i, True).wait_recv()

    def ag_drain(buf, n):
        for i in range(4):
            ag_copy(buf, n, i).wait_send()

    def pair_copy(buf, base, t, send, recv):
        ref = buf.at[t - base, upper[t]]
        return remote(ref, ref, send.at[t - base], recv.at[t - base], partners[t])

    def pair_wait(buf, base, t, send, recv):
        ref = buf.at[t - base, 1 - upper[t]]
        remote(ref, ref, send.at[t - base], recv.at[t - base], partners[t]).wait_recv()

    y_copy = pltpu.make_async_copy(ypart, ybuf, ysem)
    y_copy.start()
    rs_first(zpart, 0)
    wst[...] = dot_bx(wrow[...], subsk[...])
    rs_second(zpart, 0)
    rs_last(zpart, 0, zb)

    def compose():
        def facing(t, other):
            b = coup[t]
            low = dot_bx(b, other)
            high = dot_bx(b, other, 0, 0)
            return jnp.where(upper[t] == 1, high, low)

        def halves(t):
            own = pl.ds(pl.multiple_of(upper[t] * R, R), R)
            other = pl.ds(pl.multiple_of((1 - upper[t]) * R, R), R)
            return ub[t + 1, own, :], ub[t + 1, other, :]

        own1, other1 = halves(0)
        own2, other2 = halves(1)
        v2 = dot(own1, own2)
        c2 = -(dot(facing(0, other1), own2) + dot(own1, facing(1, other2)))
        base = ub[0]
        v = dot(base, v2)
        vbuf[col] = v
        ag_first(vbuf, 0)
        c = dot(base, c2)
        w = wrow[...]
        ps[...] = dot_xb(c, w, 0, 0)
        pp = dot_xb(v, w, 0, 0)
        for k in range(4):
            sparts[k, HIGH] = pp[:, k * R : (k + 1) * R]

    def relay_bases():
        ag_second(vbuf, 0)

    def wide_parts():
        ag_last(vbuf, 0)
        y_copy.wait()

        @pl.loop(0, 4)
        def _(k):
            rows = pl.ds(pl.multiple_of(k * 2 * R, R), 2 * R)
            ps[...] += dot(vbuf[k], ybuf[rows, :], 0, 0)

        for k in range(4):
            sparts[k, LOW] = ps[:, k * R : (k + 1) * R]
        rs_first(sparts, 1)

    def relay_parts():
        rs_second(sparts, 1)

    def wide_start():
        rs_last(sparts, 1, comm2.at[0, upper[2]])
        pair_copy(comm2, 2, 2, c2_send, c2_recv).start()

    def wide_merge(t):
        pair_wait(comm2, 2, t, c2_send, c2_recv)
        low_p, high_p = comm2[t - 2, 0, HIGH], comm2[t - 2, 1, HIGH]
        low = comm2[t - 2, 0, LOW] - dot_bx(coup[t], high_p)
        high = comm2[t - 2, 1, LOW] - dot_bx(coup[t], low_p, 0, 0)
        u_low, u_high = ub[t + 1, LOW, :], ub[t + 1, HIGH, :]
        sample = dot(u_low, low, 0, 0) + dot(u_high, high, 0, 0)
        if t == LEVELS - 1:
            topbuf[col] = sample
            return
        comm2[t - 1, upper[t + 1], LOW] = sample
        comm2[t - 1, upper[t + 1], HIGH] = dot(u_low, low_p, 0, 0) + dot(u_high, high_p, 0, 0)
        pair_copy(comm2, 2, t + 1, c2_send, c2_recv).start()

    at_start = {4: relay_parts, 5: functools.partial(wide_merge, 3)}
    at_middle = {3: relay_bases, 4: wide_start}
    at_end = {2: compose, 3: wide_parts, 4: functools.partial(wide_merge, 2)}

    def place(table, t):
        for at, piece in table.items():
            pl.when(t == at)(piece)

    i0 = lax.broadcasted_iota(jnp.int32, (16, 8, R), 0) * 8 + lax.broadcasted_iota(jnp.int32, (16, 8, R), 1)
    eye = i0 == lax.broadcasted_iota(jnp.int32, (16, 8, R), 2)

    def stage(t, carry):
        for k in range(1, LEVELS + 1):
            @pl.when(t == k)
            def _():
                pair_wait(comm, 0, k - 1, c_send, c_recv)
                b = coup[k - 1]
                low_w, high_w = comm[k - 1, 0, HIGH], comm[k - 1, 1, HIGH]
                zb[LOW] = comm[k - 1, 0, LOW] - dot_bx(b, high_w)
                zb[HIGH] = comm[k - 1, 1, LOW] - dot_bx(b, low_w, 0, 0)
                wst[LOW] = low_w
                wst[HIGH] = high_w

        place(at_start, t)
        z = zb[...]
        gram = dot(z, z, 0, 0).reshape(16, 8, R)
        shift = 0.0001 * jnp.sum(z * z, keepdims=True) / R + 1e-06
        ax[:, :, pl.ds(0, R)] = gram + jnp.where(eye, shift.reshape(1, 1, 1), 0.0)
        ax[:, :, pl.ds(R, R)] = jnp.where(eye, 1.0, 0.0)
        factor(ax, lt, lambda: place(at_middle, t))
        linv = ax[:, :, pl.ds(R, R)].reshape(R, R)
        cross = dot(z, wst[...], 0, 0)
        for k in range(LEVELS):
            @pl.when(t == k)
            def _():
                comm[k, upper[k], LOW] = lt[...] - shift * linv
                comm[k, upper[k], HIGH] = dot(linv, cross)
                pair_copy(comm, 0, k, c_send, c_recv).start()

        u = dot(z, linv, 1, 1)
        ub[t] = u

        @pl.when(t == 0)
        def _():
            leaf_out[...] = u

        for k in range(LEVELS):
            @pl.when(t == k + 1)
            def _():
                trans_out[k] = ub[t, pl.ds(pl.multiple_of(upper[k] * R, R), R), :]

        place(at_end, t)
        return carry

    lax.fori_loop(0, LEVELS + 1, stage, 0)
    wide_merge(LEVELS - 1)
    ag_first(topbuf, 1)
    ag_second(topbuf, 1)
    ag_last(topbuf, 1)
    for k in range(4):
        top_out[:, pl.ds(k * R, R)] = topbuf[k]

    rs_drain(zpart, 0)
    rs_drain(sparts, 1)
    ag_drain(vbuf, 0)
    ag_drain(topbuf, 1)
    for t in range(LEVELS):
        pair_copy(comm, 0, t, c_send, c_recv).wait_send()
    for t in range(2, LEVELS):
        pair_copy(comm2, 2, t, c2_send, c2_recv).wait_send()


def run_tree(zpart, ypart, wrow, subsketch, couplings):
    vmem = pl.BlockSpec(memory_space=pltpu.VMEM)
    hbm = pl.BlockSpec(memory_space=pl.ANY)
    dma = pltpu.SemaphoreType.DMA
    width = ypart.shape[1]

    def f32(*shape):
        return pltpu.VMEM(shape, F32)

    return pl.pallas_call(
        tree_kernel,
        out_shape=[
            jax.ShapeDtypeStruct((2 * R, R), F32),
            jax.ShapeDtypeStruct((LEVELS, R, R), F32),
            jax.ShapeDtypeStruct((R, width), F32),
        ],
        in_specs=[vmem, hbm, vmem, vmem, vmem],
        out_specs=[vmem, vmem, vmem],
        scratch_shapes=[
            f32(16, 8, 2 * R), f32(R, R), f32(2 * R, R), f32(2 * R, R), f32(LEVELS + 1, 2 * R, R),
            f32(LEVELS, 2, 2 * R, R), f32(3, 2, 2 * R, R), f32(2, 2, R, R), f32(2, 4, R, R), f32(2, 2, R, R),
            f32(4, 2 * R, R), f32(4, 2 * R, R), f32(4, R, R), f32(2 * R, R), f32(*ypart.shape), f32(R, width),
            dma((2, 6)), dma((2, 6)), dma((2, 4)), dma((2, 4)), dma((LEVELS,)), dma((LEVELS,)), dma((3,)), dma((3,)), dma,
        ],
        compiler_params=pltpu.CompilerParams(
            collective_id=0, has_side_effects=True, vmem_limit_bytes=48 * 2**20
        ),
        name="tree",
    )(zpart, ypart, wrow, subsketch, couplings)


def per_device(tiles, tile_slots, sketch, row_sketch, subsketch, couplings):
    row_tiles = row_sketch.shape[0] * lax.axis_size("col") // R
    ypart, zpart = run_sample(tiles, tile_slots, sketch, subsketch, row_tiles)
    leaf_basis, transfer, top = run_tree(
        zpart.reshape(4, 2 * R, R), ypart, row_sketch, subsketch, couplings[0]
    )
    return leaf_basis, transfer[None], top[None]


def solution(mesh):
    return jax.shard_map(
        per_device,
        mesh=mesh,
        in_specs=(
            P(("row", "col"), None, None),
            P(("row", "col")),
            P("col", None),
            P(("row", "col"), None),
            P(),
            P(("row", "col"), None, None, None),
        ),
        out_specs=(
            P(("row", "col"), None),
            P(("row", "col"), None, None, None),
            P(("row", "col"), None, None),
        ),
        check_vma=False,
    )
```

time: 423 us -> 101 us (0.24); the launches traced: 414 us -> 99.9 us
  other arithmetic: 138 us -> 0 us
  matrix products: 132 us -> 0 us
  Pallas kernels: 0 us -> 94.5 us
  waiting for transfers between devices: 76.4 us -> 0 us
  local copies, waits for them, and re-layouts: 35.2 us -> 4.72 us
  between operations: 18.7 us -> 0.71 us
  starting transfers between devices: 13.9 us -> 0 us
    another operation x31 -> x0, other arithmetic: 137 us -> none  [the longest x18 74.3 us: orthonormal(): jnp.linalg.cholesky(gram + shift * jnp.eye(gram.shape[0], dtype=jnp.float...]
    dot_general x49 -> x0, matrix products: 130 us -> none  [the longest x8 75.7 us: step(): jnp.einsum('tr,tis->ris', one_hot, product, precision=lax.Precision.HIGHEST)]
    pallas_call x0 -> x2, Pallas kernels: none -> 94.5 us  [the longest x1 72.8 us: run_tree(): pl.pallas_call(tree_kernel, out_shape=[jax.ShapeDtypeStruct((2 * R, R), F...]
    ppermute x10 -> x0, waiting for transfers between devices: 43.2 us -> none  [from_partner(): return lax.ppermute(block, axis, route)]
    reduce_scatter x1 -> x0, waiting for transfers between devices: 33.2 us -> none  [per_device(): lax.psum_scatter(partial_value, 'col', scatter_dimension=0, tiled=True)]
    gather x8 -> x0, local copies, waits for them, and re-layouts: 28.1 us -> none  [step(): picked = jnp.take(sketch_blocks, group_slots % col_tiles, axis=0)]
    ppermute x10 -> x0, starting transfers between devices: 13.9 us -> none  [from_partner(): return lax.ppermute(block, axis, route)]
  transfers between devices with their start and end apart: 11 -> 0, of which waited for: 11 -> 0; matrix products, arithmetic and copies ran while one was open for 1% -> 0% of each run, Pallas kernels for 0% -> 0%
where the time goes in v1:
time: 101 us; the launch traced here: 99.9 us
  Pallas kernels  94.5 us (94%)
  local copies, waits for them, and re-layouts  4.72 us (5%)
    pallas_call x1, Pallas kernels, run_tree(): pl.pallas_call(tree_kernel, out_shape=[jax.ShapeDtypeStruct((2 * R, R), F...  72.8 us
    pallas_call x1, Pallas kernels, run_sample(): pl.pallas_call(functools.partial(sample_kernel, 8), out_shape=[jax.ShapeD...  21.7 us
    unnamed x13, local copies, waits for them, and re-layouts  4.72 us

profile of v1, /device:TPU:192, one launch (start us, length us, event | category | flops | bytes accessed | tf_op | source)
XLA Modules:
  0.0 99.9 jit_solution(17499345753993305437)
XLA Ops:
  0.6 0.0 copy-start.1
  0.6 0.0 copy-start.3
  0.7 0.0 copy-start.4
  0.7 21.7 %sample.1 = (f32[1024,512]{1,0:T(8,128)}, f32[1024,128]{1,0:T(8,128)}) custom-call(s32[168]{0:T(256)} %slots_ref.1, bf16[168,128,128]{2,1,0:T(8,128)(2,1)} %tiles_ref.1, bf16[6144,512]{1,0:T(8,128)(2,1)} %sketch_ref.1, f32[512,128]{1,0:T(8,128)} %subsk.1), custom_call_target="tpu_custom_call" | custom-call | tf_op jit(solution)/shard_map/sample/pallas_call | solution.py:91
  22.3 0.0 copy-done.1
  22.4 0.0 copy-done.3
  22.4 0.0 copy-done.4
  22.4 0.0 copy-start
  22.4 1.6 %copy-done = f32[1024,512]{1,0:T(8,128)S(1)} copy-done((f32[1024,512]{1,0:T(8,128)S(1)}, f32[1024,512]{1,0:T(8,128)}, u32[]{:S(2)}) %copy-start) | copy-done | bytes 2097176
  24.0 0.0 copy-start.2
  24.0 1.0 %copy-done.2 = f32[1024,128]{1,0:T(8,128)S(1)} copy-done((f32[1024,128]{1,0:T(8,128)S(1)}, f32[1024,128]{1,0:T(8,128)}, u32[]{:S(2)}) %copy-start.2) | copy-done | bytes 524312
  25.0 72.8 %tree.1 = (f32[256,128]{1,0:T(8,128)S(1)}, f32[5,128,128]{2,1,0:T(8,128)S(1)}, f32[128,512]{1,0:T(8,128)S(1)}) custom-call(f32[4,256,128]{2,1,0:T(8,128)S(1)} %bitcast.4, f32[1024,512]{1,0:T(8,128)S(1)} %copy-done, bf16[256,512]{1,0:T(8,128)(2,1)S(1)} %copy-done.3, f32[512,128]{1,0:T(8,128)S(1)} %copy-done.1, bf16[5,128,128]{2,1,0:T(8,128)(2,1)S(1)} %bitcast.7), custom_call_target="tpu_custom_call" | custom-call | tf_op jit(solution)/shard_map/tree/pallas_call | solution.py:411
  97.9 0.7 copy.12
  98.5 0.7 copy.13
  99.2 0.7 copy.14
Async XLA Ops:
  0.6 21.7 %copy-start.1 = (f32[512,128]{1,0:T(8,128)S(1)}, f32[512,128]{1,0:T(8,128)}, u32[]{:S(2)}) copy-start(f32[512,128]{1,0:T(8,128)} %subsk.1) | copy-start | bytes 786436
  0.6 21.7 %copy-start.3 = (bf16[256,512]{1,0:T(8,128)(2,1)S(1)}, bf16[256,512]{1,0:T(8,128)(2,1)}, u32[]{:S(2)}) copy-start(bf16[256,512]{1,0:T(8,128)(2,1)} %wrow.1) | copy-start | bytes 786436
  0.7 21.7 %copy-start.4 = (bf16[1,5,128,128]{3,2,1,0:T(8,128)(2,1)S(1)}, bf16[1,5,128,128]{3,2,1,0:T(8,128)(2,1)}, u32[]{:S(2)}) copy-start(bf16[1,5,128,128]{3,2,1,0:T(8,128)(2,1)} %param.11) | copy-start | bytes 491524
  22.4 1.6 %copy-start = (f32[1024,512]{1,0:T(8,128)S(1)}, f32[1024,512]{1,0:T(8,128)}, u32[]{:S(2)}) copy-start(f32[1024,512]{1,0:T(8,128)} %get-tuple-element.9.ypart) | copy-start | bytes 6291460
  24.0 1.0 %copy-start.2 = (f32[1024,128]{1,0:T(8,128)S(1)}, f32[1024,128]{1,0:T(8,128)}, u32[]{:S(2)}) copy-start(f32[1024,128]{1,0:T(8,128)} %get-tuple-element.8) | copy-start | bytes 1572868

commit v2 on v1

--- a/solution.py
+++ b/solution.py
@@ -41,70 +41,6 @@
     return dot16(hi, b, ca, cb) + (dot16(mid, b, ca, cb) + dot16(low, b, ca, cb))
 
 
-def sample_kernel(step, slots_ref, tiles_ref, sketch_ref, sub_ref, y_ref, z_ref, dense, sk, present, tsem, ssem):
-    tile_count = tiles_ref.shape[0]
-    col_tiles = dense.shape[0]
-    row_tiles = dense.shape[1] // R
-    sketch_copy = pltpu.make_async_copy(sketch_ref, sk, ssem)
-    sketch_copy.start()
-
-    @pl.loop(0, present.shape[0], unroll=8)
-    def _(v):
-        present[v] = 0
-
-    @pl.loop(0, tile_count, unroll=4)
-    def _(t):
-        v = slots_ref[t]
-        present[v] = 1
-        r = v // col_tiles
-        rows = pl.ds(pl.multiple_of(r * R, R), R)
-        pltpu.make_async_copy(tiles_ref.at[t], dense.at[v - r * col_tiles, rows, :], tsem).start()
-
-    zero = jnp.zeros((R, R), BF)
-
-    @pl.loop(0, present.shape[0])
-    def _(v):
-        @pl.when(present[v] == 0)
-        def _():
-            r = v // col_tiles
-            dense[v - r * col_tiles, pl.ds(pl.multiple_of(r * R, R), R), :] = zero
-
-    sketch_copy.wait()
-    arrived = dense.at[pl.ds(0, tile_count // row_tiles)]
-    pltpu.make_async_copy(arrived, arrived, tsem).wait()
-    y_ref[...] = jnp.zeros_like(y_ref)
-
-    @pl.loop(0, col_tiles // step)
-    def _(p):
-        lhs = jnp.concatenate([dense[p * step + i] for i in range(step)], axis=1)
-        rhs = sk[pl.ds(pl.multiple_of(p * step * R, R), step * R), :]
-        y_ref[...] += jnp.dot(lhs, rhs, preferred_element_type=F32)
-
-    z_ref[...] = dot(y_ref[...], sub_ref[...])
-
-
-def run_sample(tiles, slots, sketch, subsketch, row_tiles):
-    col_tiles = sketch.shape[0] // R
-    rows, width = row_tiles * R, sketch.shape[1]
-    vmem = pl.BlockSpec(memory_space=pltpu.VMEM)
-    hbm = pl.BlockSpec(memory_space=pl.ANY)
-    return pl.pallas_call(
-        functools.partial(sample_kernel, 8),
-        out_shape=[jax.ShapeDtypeStruct((rows, width), F32), jax.ShapeDtypeStruct((rows, R), F32)],
-        in_specs=[pl.BlockSpec(memory_space=pltpu.SMEM), hbm, hbm, vmem],
-        out_specs=[vmem, vmem],
-        scratch_shapes=[
-            pltpu.VMEM((col_tiles, rows, R), BF),
-            pltpu.VMEM(sketch.shape, BF),
-            pltpu.SMEM((row_tiles * col_tiles,), jnp.int32),
-            pltpu.SemaphoreType.DMA,
-            pltpu.SemaphoreType.DMA,
-        ],
-        compiler_params=pltpu.CompilerParams(vmem_limit_bytes=60 * 2**20),
-        name="sample",
-    )(slots, tiles, sketch, subsketch)
-
-
 def row_of(x, k):
     return jnp.broadcast_to(x[k : k + 1, :], x.shape)
 
@@ -115,7 +51,7 @@
     for j in range(blocks):
         if j == blocks // 2:
             middle()
-        own = ax[j]
+        own = ax[j] if j == 0 else following
         cols = [jnp.broadcast_to(own[:, 8 * j + k : 8 * j + k + 1], (8, R)) for k in range(8)]
         d = [[row_of(cols[k], i) if i >= k else None for k in range(8)] for i in range(8)]
         rows = [row_of(own, k) for k in range(8)]
@@ -150,15 +86,53 @@
                 terms.append(c * q[k])
             while len(terms) > 1:
                 terms = [terms[i] + terms[i + 1] for i in range(0, len(terms), 2)]
-            ax[g] = rest - terms[0]
+            rest = rest - terms[0]
+            if g == j + 1:
+                following = rest
+            else:
+                ax[g] = rest
 
 
 def tree_kernel(
-    zpart, ypart, wrow, subsk, coup,
+    slots, tiles_hbm, sketch_hbm, wrow_hbm, subsk_hbm, coup_hbm,
     leaf_out, trans_out, top_out,
-    ax, lt, zb, wst, ub, comm, comm2, relay, fin, staged, sparts, vbuf, topbuf, cbuf, ybuf, ps,
-    rs_send, rs_recv, ag_send, ag_recv, c_send, c_recv, c2_send, c2_recv, ysem,
+    tiles, sketch, wrow, subsk, coup, slot_pad, index_row, index,
+    ax, lt, zb, wst, ub, comm, comm2, relay, fin, staged, zparts, sparts, vbuf, topbuf, ybuf, ps,
+    rs_send, rs_recv, ag_send, ag_recv, c_send, c_recv, c2_send, c2_recv, t_sem, k_sem, i_sem, n_sem,
 ):
+    tile_count = tiles_hbm.shape[0]
+    col_tiles = sketch_hbm.shape[0] // R
+
+    def load(src, dst, sem):
+        copy = pltpu.make_async_copy(src, dst, sem)
+        copy.start()
+        return copy
+
+    small = [
+        load(src, dst, i_sem.at[i])
+        for i, (src, dst) in enumerate([(wrow_hbm, wrow), (subsk_hbm, subsk)])
+    ]
+    per = tile_count // t_sem.shape[0]
+    tile_copies = [
+        load(tiles_hbm.at[pl.ds(i * per, per)], tiles.at[pl.ds(i * per, per)], t_sem.at[i])
+        for i in range(t_sem.shape[0])
+    ]
+    chunk = sketch_hbm.shape[0] // k_sem.shape[0]
+    for i in range(k_sem.shape[0]):
+        load(sketch_hbm.at[pl.ds(i * chunk, chunk)], sketch.at[pl.ds(i * chunk, chunk)], k_sem.at[i])
+    small.append(load(coup_hbm, coup, i_sem.at[2]))
+
+    slot_pad[...] = jnp.full_like(slot_pad, -1)
+    slot_pad[pl.ds(0, 1), pl.ds(0, tile_count)] = slots[...]
+    by_tile = jnp.broadcast_to(slot_pad[pl.ds(0, 1), :], (R, slot_pad.shape[1])).T
+    which = jnp.minimum(lax.broadcasted_iota(jnp.int32, by_tile.shape, 0), tile_count)
+    lane = lax.broadcasted_iota(jnp.int32, by_tile.shape, 1)
+    for i in range(index_row.shape[1] // R):
+        found = jnp.where(by_tile == lane + i * R, which, tile_count)
+        index_row[:, pl.ds(i * R, R)] = jnp.min(found, axis=0, keepdims=True)
+    index_copy = load(index_row, index, n_sem)
+    tiles[tile_count] = jnp.zeros((R, R), BF)
+
     row, col = lax.axis_index("row"), lax.axis_index("col")
     position = row * 4 + col
     right, left = (col + 1) % 4, (col + 3) % 4
@@ -256,12 +230,50 @@
         ref = buf.at[t - base, 1 - upper[t]]
         remote(ref, ref, send.at[t - base], recv.at[t - base], partners[t]).wait_recv()
 
-    y_copy = pltpu.make_async_copy(ypart, ybuf, ysem)
-    y_copy.start()
-    rs_first(zpart, 0)
+    def leaf_rows(leaf):
+        return pl.ds(pl.multiple_of(leaf * 2 * R, R), 2 * R)
+
+    def block_rows(leaf, first, count):
+        return jnp.concatenate(
+            [
+                jnp.concatenate([tiles[index[0, (2 * leaf + i) * col_tiles + first + k]] for k in range(count)], axis=1)
+                for i in range(2)
+            ],
+            axis=0,
+        )
+
+    def partial_samples(leaves, count, arriving):
+        for leaf in leaves:
+            ybuf[leaf_rows(leaf), :] = jnp.zeros((2 * R, ybuf.shape[1]), F32)
+
+        @pl.loop(0, col_tiles // count)
+        def _(p):
+            rows = pl.ds(pl.multiple_of(p * count * R, R), count * R)
+            if arriving:
+                pltpu.make_async_copy(sketch_hbm.at[rows], sketch.at[rows], k_sem.at[p]).wait()
+            lhs = jnp.concatenate([block_rows(leaf, p * count, count) for leaf in leaves], axis=0)
+            product = dot16(lhs, sketch[rows, :])
+            for i, leaf in enumerate(leaves):
+                ybuf[leaf_rows(leaf), :] += product[i * 2 * R : (i + 1) * 2 * R]
+
+        for leaf in leaves:
+            zparts[leaf] = dot(ybuf[leaf_rows(leaf), :], subsk[...])
+
+    small[0].wait()
+    small[1].wait()
     wst[...] = dot_bx(wrow[...], subsk[...])
-    rs_second(zpart, 0)
-    rs_last(zpart, 0, zb)
+    index_copy.wait()
+    for copy in tile_copies:
+        copy.wait()
+    partial_samples([across, right], col_tiles // k_sem.shape[0], True)
+    for i in range(3):
+        rs_copy(zparts, 0, i).start()
+    partial_samples([left], 8, False)
+    rs_copy(zparts, 0, 3).start()
+    rs_second(zparts, 0)
+    partial_samples([col], 8, False)
+    small[2].wait()
+    rs_last(zparts, 0, zb)
 
     def compose():
         def facing(t, other):
@@ -295,7 +307,6 @@
 
     def wide_parts():
         ag_last(vbuf, 0)
-        y_copy.wait()
 
         @pl.loop(0, 4)
         def _(k):
@@ -389,7 +400,7 @@
     for k in range(4):
         top_out[:, pl.ds(k * R, R)] = topbuf[k]
 
-    rs_drain(zpart, 0)
+    rs_drain(zparts, 0)
     rs_drain(sparts, 1)
     ag_drain(vbuf, 0)
     ag_drain(topbuf, 1)
@@ -399,11 +410,13 @@
         pair_copy(comm2, 2, t, c2_send, c2_recv).wait_send()
 
 
-def run_tree(zpart, ypart, wrow, subsketch, couplings):
+def run_tree(slots, tiles, sketch, wrow, subsketch, couplings):
     vmem = pl.BlockSpec(memory_space=pltpu.VMEM)
-    hbm = pl.BlockSpec(memory_space=pl.ANY)
+    hbm = pl.BlockSpec(memory_space=pltpu.HBM)
     dma = pltpu.SemaphoreType.DMA
-    width = ypart.shape[1]
+    tile_count = tiles.shape[0]
+    depth, width = sketch.shape
+    slot_count = 8 * depth // R
 
     def f32(*shape):
         return pltpu.VMEM(shape, F32)
@@ -415,26 +428,28 @@
             jax.ShapeDtypeStruct((LEVELS, R, R), F32),
             jax.ShapeDtypeStruct((R, width), F32),
         ],
-        in_specs=[vmem, hbm, vmem, vmem, vmem],
+        in_specs=[vmem, hbm, hbm, hbm, hbm, hbm],
         out_specs=[vmem, vmem, vmem],
         scratch_shapes=[
+            pltpu.VMEM((tile_count + 1, R, R), BF), pltpu.VMEM((depth, width), BF), pltpu.VMEM(wrow.shape, BF),
+            f32(width, R), pltpu.VMEM(couplings.shape, BF), pltpu.VMEM((1, 2 * R), jnp.int32),
+            pltpu.VMEM((1, slot_count), jnp.int32), pltpu.SMEM((1, slot_count), jnp.int32),
             f32(16, 8, 2 * R), f32(R, R), f32(2 * R, R), f32(2 * R, R), f32(LEVELS + 1, 2 * R, R),
             f32(LEVELS, 2, 2 * R, R), f32(3, 2, 2 * R, R), f32(2, 2, R, R), f32(2, 4, R, R), f32(2, 2, R, R),
-            f32(4, 2 * R, R), f32(4, 2 * R, R), f32(4, R, R), f32(2 * R, R), f32(*ypart.shape), f32(R, width),
-            dma((2, 6)), dma((2, 6)), dma((2, 4)), dma((2, 4)), dma((LEVELS,)), dma((LEVELS,)), dma((3,)), dma((3,)), dma,
+            f32(4, 2 * R, R), f32(4, 2 * R, R), f32(4, 2 * R, R), f32(4, R, R), f32(8 * R, width), f32(R, width),
+            dma((2, 6)), dma((2, 6)), dma((2, 4)), dma((2, 4)), dma((LEVELS,)), dma((LEVELS,)), dma((3,)), dma((3,)),
+            dma((4,)), dma((12,)), dma((3,)), dma,
         ],
         compiler_params=pltpu.CompilerParams(
-            collective_id=0, has_side_effects=True, vmem_limit_bytes=48 * 2**20
+            collective_id=0, has_side_effects=True, vmem_limit_bytes=66_300_000
         ),
         name="tree",
-    )(zpart, ypart, wrow, subsketch, couplings)
+    )(slots, tiles, sketch, wrow, subsketch, couplings)
 
 
 def per_device(tiles, tile_slots, sketch, row_sketch, subsketch, couplings):
-    row_tiles = row_sketch.shape[0] * lax.axis_size("col") // R
-    ypart, zpart = run_sample(tiles, tile_slots, sketch, subsketch, row_tiles)
     leaf_basis, transfer, top = run_tree(
-        zpart.reshape(4, 2 * R, R), ypart, row_sketch, subsketch, couplings[0]
+        tile_slots.reshape(1, -1), tiles, sketch, row_sketch, subsketch, couplings[0]
     )
     return leaf_basis, transfer[None], top[None]
 

time: 101 us -> 89.7 us (0.89)
  Pallas kernels: 94.5 us -> 83.1 us
    pallas_call x1 -> x0, Pallas kernels: 21.7 us -> none  [run_sample(): pl.pallas_call(functools.partial(sample_kernel, 8), out_shape=[jax.ShapeD...]
    pallas_call x1, Pallas kernels: 72.8 us -> 83.1 us  [run_tree(): pl.pallas_call(tree_kernel, out_shape=[jax.ShapeDtypeStruct((2 * R, R), F...]
    unnamed x13 -> x3, local copies, waits for them, and re-layouts: 4.72 us -> 4.96 us
where the time goes in v2:
time: 89.7 us; the launch traced here: 88.7 us
  Pallas kernels  83.1 us (93%)
  local copies, waits for them, and re-layouts  4.96 us (6%)
    pallas_call x1, Pallas kernels, run_tree(): pl.pallas_call(tree_kernel, out_shape=[jax.ShapeDtypeStruct((2 * R, R), F...  83.1 us
    unnamed x3, local copies, waits for them, and re-layouts  4.96 us

profile of v2, /device:TPU:192, one launch (start us, length us, event | category | flops | bytes accessed | tf_op | source)
XLA Modules:
  0.0 88.7 jit_solution(2472086454771228800)
XLA Ops:
  0.6 83.1 %tree.1 = (f32[256,128]{1,0:T(8,128)}, f32[5,128,128]{2,1,0:T(8,128)}, f32[128,512]{1,0:T(8,128)}) custom-call(s32[1,168]{1,0:T(1,128)} %bitcast.7, bf16[168,128,128]{2,1,0:T(8,128)(2,1)} %tiles_hbm.1, bf16[6144,512]{1,0:T(8,128)(2,1)} %sketch_hbm.1, bf16[256,512]{1,0:T(8,128)(2,1)} %wrow_hbm.1, f32[512,128]{1,0:T(8,128)} %subsk_hbm.1, ...), custom_call_target="tpu_custom_call" | custom-call | tf_op jit(solution)/shard_map/tree/pallas_call | solution.py:424
  83.8 1.6 %copy.12 = f32[256,128]{1,0:T(8,128)} copy(f32[256,128]{1,0:T(8,128)} %get-tuple-element.12) | data formatting | bytes 262144
  85.4 1.7 %copy.13 = f32[1,5,128,128]{3,2,1,0:T(8,128)} copy(f32[1,5,128,128]{3,2,1,0:T(8,128)} %bitcast.4) | data formatting | bytes 655360
  87.1 1.7 %copy.14 = f32[1,128,512]{2,1,0:T(8,128)} copy(f32[1,128,512]{2,1,0:T(8,128)} %bitcast.5) | data formatting | bytes 524288

commit v3 on v2

--- a/solution.py
+++ b/solution.py
@@ -45,59 +45,72 @@
     return jnp.broadcast_to(x[k : k + 1, :], x.shape)
 
 
-def factor(ax, lt, middle):
-    blocks = ax.shape[0]
-    sub = lax.broadcasted_iota(jnp.int32, (8, 2 * R), 0)
-    for j in range(blocks):
-        if j == blocks // 2:
-            middle()
-        own = ax[j] if j == 0 else following
-        cols = [jnp.broadcast_to(own[:, 8 * j + k : 8 * j + k + 1], (8, R)) for k in range(8)]
+def lane_of(x, k):
+    return jnp.broadcast_to(x[:, k : k + 1], x.shape)
+
+
+def factor(t_ref, x_ref, one, segment):
+    n = t_ref.shape[0]
+    sub = lax.broadcasted_iota(jnp.int32, (8, 128), 0)
+    lane = lax.broadcasted_iota(jnp.int32, (8, 128), 1)
+    following = t_ref[0]
+    cols = [lane_of(following, k) * one for k in range(8)]
+    for j in range(n):
+        segment(j)
+        base = 8 * j
+        block = jnp.where(lane == sub + base, 1.0, jnp.where((lane >= base) & (lane < base + 8), 0.0, following))
+        rows = [row_of(block, k) for k in range(8)]
         d = [[row_of(cols[k], i) if i >= k else None for k in range(8)] for i in range(8)]
-        rows = [row_of(own, k) for k in range(8)]
-        inv, mult = [], [[None] * 8 for _ in range(8)]
+        last = j == n - 1
+        if not last:
+            nxt = t_ref[j + 1]
+            c = [lane_of(nxt, base + k) * one for k in range(8)]
+            following = jnp.where((lane >= base) & (lane < base + 8), 0.0, nxt)
+            ncols = [lane_of(nxt, base + 8 + k) for k in range(8)]
+        inv = []
+        mult = [[None] * 8 for _ in range(8)]
         for k in range(8):
-            inv.append(1.0 / d[k][k])
+            iv = 1.0 / d[k][k]
+            inv.append(iv)
             for i in range(k + 1, 8):
-                m = d[i][k] * inv[k]
-                mult[i][k] = jnp.concatenate([m, m], axis=1)
+                m = d[i][k] * iv
+                mult[i][k] = m
                 for i2 in range(i, 8):
                     d[i2][i] = d[i2][i] - d[i2][k] * m
-                rows[i] = rows[i] - mult[i][k] * rows[k]
-        out = rows[0]
-        pivots = d[0][0]
+                rows[i] = rows[i] - m * rows[k]
+                if not last:
+                    c[i] = c[i] - m * c[k]
+            if not last:
+                e = c[k] * iv
+                for k2 in range(8):
+                    ncols[k2] = ncols[k2] - e * row_of(c[k], k2)
+                following = following - e * rows[k]
+        out, pivots = rows[0], d[0][0]
         for k in range(1, 8):
             out = jnp.where(sub == k, rows[k], out)
-            pivots = jnp.where(sub[:, :R] == k, d[k][k], pivots)
-        scale = lax.rsqrt(pivots)
-        lt[pl.ds(8 * j, 8), :] = out[:, :R] * scale
-        ax[j, :, pl.ds(R, R)] = out[:, R:] * scale
-        if j == blocks - 1:
+            pivots = jnp.where(sub == k, d[k][k], pivots)
+        x_ref[pl.ds(base, 8), :] = jnp.where(lane < base + 8, out * lax.rsqrt(pivots), 0.0)
+        if last:
             break
-        q = [rows[k] * jnp.concatenate([inv[k], inv[k]], axis=1) for k in range(8)]
-        for k in range(7, 0, -1):
-            for i in range(k):
-                q[i] = q[i] - mult[k][i] * q[k]
-        for g in range(j + 1, blocks):
-            rest = ax[g]
-            terms = []
-            for k in range(8):
-                c = jnp.broadcast_to(rest[:, 8 * j + k : 8 * j + k + 1], (8, 2 * R))
-                terms.append(c * q[k])
-            while len(terms) > 1:
-                terms = [terms[i] + terms[i + 1] for i in range(0, len(terms), 2)]
-            rest = rest - terms[0]
-            if g == j + 1:
-                following = rest
-            else:
-                ax[g] = rest
+        cols = ncols
+        if j < n - 2:
+            q = [rows[k] * inv[k] for k in range(8)]
+            for k in range(7, 0, -1):
+                for i in range(k):
+                    q[i] = q[i] - mult[k][i] * q[k]
+            for g in range(j + 2, n):
+                rest = t_ref[g]
+                terms = [lane_of(rest, base + k) * q[k] for k in range(8)]
+                while len(terms) > 1:
+                    terms = [terms[i] + terms[i + 1] for i in range(0, len(terms), 2)]
+                t_ref[g] = jnp.where((lane >= base) & (lane < base + 8), 0.0, rest) - terms[0]
 
 
 def tree_kernel(
-    slots, tiles_hbm, sketch_hbm, wrow_hbm, subsk_hbm, coup_hbm,
+    slots_hbm, tiles_hbm, sketch_hbm, wrow_hbm, subsk_hbm, coup_hbm,
     leaf_out, trans_out, top_out,
-    tiles, sketch, wrow, subsk, coup, slot_pad, index_row, index,
-    ax, lt, zb, wst, ub, comm, comm2, relay, fin, staged, zparts, sparts, vbuf, topbuf, ybuf, ps,
+    slots, tiles, sketch, wrow, subsk, coup, slot_pad, index_row, index,
+    work, linv, gm, zw, ub, comm, comm2, relay, fin, staged, zparts, sparts, vbuf, topbuf, ybuf, ps,
     rs_send, rs_recv, ag_send, ag_recv, c_send, c_recv, c2_send, c2_recv, t_sem, k_sem, i_sem, n_sem,
 ):
     tile_count = tiles_hbm.shape[0]
@@ -110,7 +123,7 @@
 
     small = [
         load(src, dst, i_sem.at[i])
-        for i, (src, dst) in enumerate([(wrow_hbm, wrow), (subsk_hbm, subsk)])
+        for i, (src, dst) in enumerate([(slots_hbm, slots), (wrow_hbm, wrow), (subsk_hbm, subsk)])
     ]
     per = tile_count // t_sem.shape[0]
     tile_copies = [
@@ -118,11 +131,15 @@
         for i in range(t_sem.shape[0])
     ]
     chunk = sketch_hbm.shape[0] // k_sem.shape[0]
-    for i in range(k_sem.shape[0]):
-        load(sketch_hbm.at[pl.ds(i * chunk, chunk)], sketch.at[pl.ds(i * chunk, chunk)], k_sem.at[i])
-    small.append(load(coup_hbm, coup, i_sem.at[2]))
+
+    def load_sketch(first, last):
+        for i in range(first, last):
+            load(sketch_hbm.at[pl.ds(i * chunk, chunk)], sketch.at[pl.ds(i * chunk, chunk)], k_sem.at[i])
+
+    load_sketch(0, 2)
 
     slot_pad[...] = jnp.full_like(slot_pad, -1)
+    small[0].wait()
     slot_pad[pl.ds(0, 1), pl.ds(0, tile_count)] = slots[...]
     by_tile = jnp.broadcast_to(slot_pad[pl.ds(0, 1), :], (R, slot_pad.shape[1])).T
     which = jnp.minimum(lax.broadcasted_iota(jnp.int32, by_tile.shape, 0), tile_count)
@@ -189,8 +206,8 @@
     def rs_last(parts, n, out):
         for i in range(2, 6):
             rs_copy(parts, n, i).wait_recv()
-        out[LOW] = parts[col, LOW] + (fin[n, 0] + fin[n, 2])
-        out[HIGH] = parts[col, HIGH] + (fin[n, 1] + fin[n, 3])
+        out[LOW, :] = parts[col, LOW] + (fin[n, 0] + fin[n, 2])
+        out[HIGH, :] = parts[col, HIGH] + (fin[n, 1] + fin[n, 3])
 
     def rs_drain(parts, n):
         for i in range(6):
@@ -259,21 +276,23 @@
         for leaf in leaves:
             zparts[leaf] = dot(ybuf[leaf_rows(leaf), :], subsk[...])
 
-    small[0].wait()
     small[1].wait()
-    wst[...] = dot_bx(wrow[...], subsk[...])
+    small[2].wait()
+    zw[:, HIGH] = dot_bx(wrow[...], subsk[...])
     index_copy.wait()
     for copy in tile_copies:
         copy.wait()
+    load_sketch(2, k_sem.shape[0])
+    small.append(load(coup_hbm, coup, i_sem.at[3]))
     partial_samples([across, right], col_tiles // k_sem.shape[0], True)
     for i in range(3):
         rs_copy(zparts, 0, i).start()
-    partial_samples([left], 8, False)
+    partial_samples([left], 16, False)
     rs_copy(zparts, 0, 3).start()
     rs_second(zparts, 0)
-    partial_samples([col], 8, False)
-    small[2].wait()
-    rs_last(zparts, 0, zb)
+    partial_samples([col], 16, False)
+    small[3].wait()
+    rs_last(zparts, 0, zw.at[:, LOW])
 
     def compose():
         def facing(t, other):
@@ -348,46 +367,72 @@
 
     i0 = lax.broadcasted_iota(jnp.int32, (16, 8, R), 0) * 8 + lax.broadcasted_iota(jnp.int32, (16, 8, R), 1)
     eye = i0 == lax.broadcasted_iota(jnp.int32, (16, 8, R), 2)
+    one = jnp.broadcast_to(jnp.where(position >= 0, 1.0, 0.0).astype(F32), (8, R))
+    pieces = 4
+    piece = R // pieces
+
+    def of_level(t, values):
+        return sum(jnp.where(t == k, value, 0) for k, value in enumerate(values))
 
     def stage(t, carry):
-        for k in range(1, LEVELS + 1):
-            @pl.when(t == k)
+        own = of_level(t, upper)
+        peer = (of_level(t, [p[0] for p in partners]), of_level(t, [p[1] for p in partners]))
+        below = t - 1
+
+        def piece_copy(level, side, i):
+            ref = comm.at[level, side, pl.ds(i * piece, piece), :]
+            return remote(ref, ref, c_send.at[level, i], c_recv.at[level, i], peer)
+
+        @pl.when(t > 0)
+        def _():
+            own_below = of_level(below, upper)
+            for i in range(pieces):
+                piece_copy(below, 1 - own_below, i).wait_recv()
+            b = coup[below]
+            low_w, high_w = comm[below, 0, :, HIGH], comm[below, 1, :, HIGH]
+            zw[LOW, LOW] = comm[below, 0, :, LOW] - dot_bx(b, high_w)
+            zw[HIGH, LOW] = comm[below, 1, :, LOW] - dot_bx(b, low_w, 0, 0)
+            zw[LOW, HIGH] = low_w
+            zw[HIGH, HIGH] = high_w
+
+        place(at_start, t)
+        z = zw[:, LOW]
+        products = dot(z, zw[...], 0, 0)
+        gm[...] = products
+        shift = 0.0001 * jnp.sum(z * z, keepdims=True) / R + 1e-06
+        work[...] = products[:, :R].reshape(16, 8, R) + jnp.where(eye, shift.reshape(1, 1, 1), 0.0)
+
+        def make_piece(i):
+            rows = pl.ds(i * piece, piece)
+            comm[t, own, rows, :] = dot(linv[rows, :], gm[...])
+
+        def send_piece(i):
+            @pl.when(t < LEVELS)
             def _():
-                pair_wait(comm, 0, k - 1, c_send, c_recv)
-                b = coup[k - 1]
-                low_w, high_w = comm[k - 1, 0, HIGH], comm[k - 1, 1, HIGH]
-                zb[LOW] = comm[k - 1, 0, LOW] - dot_bx(b, high_w)
-                zb[HIGH] = comm[k - 1, 1, LOW] - dot_bx(b, low_w, 0, 0)
-                wst[LOW] = low_w
-                wst[HIGH] = high_w
-
-        place(at_start, t)
-        z = zb[...]
-        gram = dot(z, z, 0, 0).reshape(16, 8, R)
-        shift = 0.0001 * jnp.sum(z * z, keepdims=True) / R + 1e-06
-        ax[:, :, pl.ds(0, R)] = gram + jnp.where(eye, shift.reshape(1, 1, 1), 0.0)
-        ax[:, :, pl.ds(R, R)] = jnp.where(eye, 1.0, 0.0)
-        factor(ax, lt, lambda: place(at_middle, t))
-        linv = ax[:, :, pl.ds(R, R)].reshape(R, R)
-        cross = dot(z, wst[...], 0, 0)
-        for k in range(LEVELS):
-            @pl.when(t == k)
-            def _():
-                comm[k, upper[k], LOW] = lt[...] - shift * linv
-                comm[k, upper[k], HIGH] = dot(linv, cross)
-                pair_copy(comm, 0, k, c_send, c_recv).start()
-
-        u = dot(z, linv, 1, 1)
+                piece_copy(t, own, i).start()
+
+        def segment(j):
+            if j == 8:
+                place(at_middle, t)
+            if j % 4 == 2 and j > 4:
+                send_piece(j // 4 - 1)
+            if j % 4 == 0 and j > 0:
+                make_piece(j // 4 - 1)
+
+        factor(work, linv, one, segment)
+        make_piece(pieces - 1)
+        send_piece(pieces - 1)
+        u = dot(zw[:, LOW], linv[...], 1, 1)
         ub[t] = u
 
         @pl.when(t == 0)
         def _():
             leaf_out[...] = u
 
-        for k in range(LEVELS):
-            @pl.when(t == k + 1)
-            def _():
-                trans_out[k] = ub[t, pl.ds(pl.multiple_of(upper[k] * R, R), R), :]
+        @pl.when(t > 0)
+        def _():
+            half = pl.ds(pl.multiple_of(of_level(below, upper) * R, R), R)
+            trans_out[below] = ub[t, half, :]
 
         place(at_end, t)
         return carry
@@ -405,7 +450,9 @@
     ag_drain(vbuf, 0)
     ag_drain(topbuf, 1)
     for t in range(LEVELS):
-        pair_copy(comm, 0, t, c_send, c_recv).wait_send()
+        for i in range(pieces):
+            ref = comm.at[t, upper[t], pl.ds(i * piece, piece), :]
+            remote(ref, ref, c_send.at[t, i], c_recv.at[t, i], partners[t]).wait_send()
     for t in range(2, LEVELS):
         pair_copy(comm2, 2, t, c2_send, c2_recv).wait_send()
 
@@ -428,23 +475,23 @@
             jax.ShapeDtypeStruct((LEVELS, R, R), F32),
             jax.ShapeDtypeStruct((R, width), F32),
         ],
-        in_specs=[vmem, hbm, hbm, hbm, hbm, hbm],
+        in_specs=[hbm] * 6,
         out_specs=[vmem, vmem, vmem],
         scratch_shapes=[
-            pltpu.VMEM((tile_count + 1, R, R), BF), pltpu.VMEM((depth, width), BF), pltpu.VMEM(wrow.shape, BF),
+            pltpu.VMEM(slots.shape, jnp.int32), pltpu.VMEM((tile_count + 1, R, R), BF), pltpu.VMEM((depth, width), BF), pltpu.VMEM(wrow.shape, BF),
             f32(width, R), pltpu.VMEM(couplings.shape, BF), pltpu.VMEM((1, 2 * R), jnp.int32),
             pltpu.VMEM((1, slot_count), jnp.int32), pltpu.SMEM((1, slot_count), jnp.int32),
-            f32(16, 8, 2 * R), f32(R, R), f32(2 * R, R), f32(2 * R, R), f32(LEVELS + 1, 2 * R, R),
-            f32(LEVELS, 2, 2 * R, R), f32(3, 2, 2 * R, R), f32(2, 2, R, R), f32(2, 4, R, R), f32(2, 2, R, R),
+            f32(16, 8, R), f32(R, R), f32(R, 2 * R), f32(2 * R, 2 * R), f32(LEVELS + 1, 2 * R, R),
+            f32(LEVELS + 1, 2, R, 2 * R), f32(3, 2, 2 * R, R), f32(2, 2, R, R), f32(2, 4, R, R), f32(2, 2, R, R),
             f32(4, 2 * R, R), f32(4, 2 * R, R), f32(4, 2 * R, R), f32(4, R, R), f32(8 * R, width), f32(R, width),
-            dma((2, 6)), dma((2, 6)), dma((2, 4)), dma((2, 4)), dma((LEVELS,)), dma((LEVELS,)), dma((3,)), dma((3,)),
-            dma((4,)), dma((12,)), dma((3,)), dma,
+            dma((2, 6)), dma((2, 6)), dma((2, 4)), dma((2, 4)), dma((LEVELS, 4)), dma((LEVELS, 4)), dma((3,)), dma((3,)),
+            dma((4,)), dma((6,)), dma((4,)), dma,
         ],
         compiler_params=pltpu.CompilerParams(
-            collective_id=0, has_side_effects=True, vmem_limit_bytes=66_300_000
+            collective_id=0, has_side_effects=True, vmem_limit_bytes=48 * 2**20
         ),
         name="tree",
-    )(slots, tiles, sketch, wrow, subsketch, couplings)
+    )(*[pltpu.with_memory_space_constraint(a, pltpu.HBM) for a in (slots, tiles, sketch, wrow, subsketch, couplings)])
 
 
 def per_device(tiles, tile_slots, sketch, row_sketch, subsketch, couplings):

time: 89.7 us -> 76.3 us (0.85)
  Pallas kernels: 83.1 us -> 72.7 us
  local copies, waits for them, and re-layouts: 4.96 us -> 2.08 us
    pallas_call x1, Pallas kernels: 83.1 us -> 72.7 us  [run_tree(): pl.pallas_call(tree_kernel, out_shape=[jax.ShapeDtypeStruct((2 * R, R), F...]
    unnamed x3, local copies, waits for them, and re-layouts: 4.96 us -> 2.08 us
where the time goes in v3:
time: 76.3 us; the launch traced here: 75.4 us
  Pallas kernels  72.7 us (95%)
  local copies, waits for them, and re-layouts  2.08 us (3%)
    pallas_call x1, Pallas kernels, run_tree(): pl.pallas_call(tree_kernel, out_shape=[jax.ShapeDtypeStruct((2 * R, R), F...  72.7 us
    unnamed x3, local copies, waits for them, and re-layouts  2.08 us

profile of v3, /device:TPU:192, one launch (start us, length us, event | category | flops | bytes accessed | tf_op | source)
XLA Modules:
  0.0 75.4 jit_solution(4027377382626473781)
XLA Ops:
  0.6 72.7 %tree.1 = (f32[256,128]{1,0:T(8,128)S(1)}, f32[5,128,128]{2,1,0:T(8,128)S(1)}, f32[128,512]{1,0:T(8,128)S(1)}) custom-call(s32[1,168]{1,0:T(1,128)} %bitcast.7, bf16[168,128,128]{2,1,0:T(8,128)(2,1)} %tiles_hbm.1, bf16[6144,512]{1,0:T(8,128)(2,1)} %sketch_hbm.1, bf16[256,512]{1,0:T(8,128)(2,1)} %wrow_hbm.1, f32[512,128]{1,0:T(8,128)} %subsk_hbm.1, ...), custom_call_target="tpu_custom_call" | custom-call | tf_op jit(solution)/shard_map/tree/pallas_call | solution.py:471
  73.3 0.7 copy.12
  74.0 0.7 copy.13
  74.7 0.7 copy.14

commit v4 on v3

--- a/solution.py
+++ b/solution.py
@@ -110,8 +110,8 @@
     slots_hbm, tiles_hbm, sketch_hbm, wrow_hbm, subsk_hbm, coup_hbm,
     leaf_out, trans_out, top_out,
     slots, tiles, sketch, wrow, subsk, coup, slot_pad, index_row, index,
-    work, linv, gm, zw, ub, comm, comm2, relay, fin, staged, zparts, sparts, vbuf, topbuf, ybuf, ps,
-    rs_send, rs_recv, ag_send, ag_recv, c_send, c_recv, c2_send, c2_recv, t_sem, k_sem, i_sem, n_sem,
+    work, linv, gm, zw, ub, comm, comm2, relay, fin, staged, zparts, sparts, vbuf, topbuf, ybuf, p0, s0, u1, down,
+    rs_send, rs_recv, ag_send, ag_recv, c_send, c_recv, c2_send, c2_recv, u_send, u_recv, t_sem, k_sem, i_sem, n_sem,
 ):
     tile_count = tiles_hbm.shape[0]
     col_tiles = sketch_hbm.shape[0] // R
@@ -284,56 +284,62 @@
         copy.wait()
     load_sketch(2, k_sem.shape[0])
     small.append(load(coup_hbm, coup, i_sem.at[3]))
-    partial_samples([across, right], col_tiles // k_sem.shape[0], True)
-    for i in range(3):
+    partial_samples([across], col_tiles // k_sem.shape[0], True)
+    for i in range(2):
         rs_copy(zparts, 0, i).start()
-    partial_samples([left], 16, False)
-    rs_copy(zparts, 0, 3).start()
+    partial_samples([right, left], 8, False)
+    for i in range(2, 4):
+        rs_copy(zparts, 0, i).start()
     rs_second(zparts, 0)
     partial_samples([col], 16, False)
     small[3].wait()
     rs_last(zparts, 0, zw.at[:, LOW])
 
-    def compose():
+    def share_leaf():
+        vbuf[col] = ub[0]
+        ag_first(vbuf, 0)
+        p0[...] = dot_xb(ub[0], wrow[...], 0, 0)
+
+    def leaf_part(leaf):
+        rows = pl.ds(pl.multiple_of(leaf * R, R), R)
+        s0[rows, :] = dot(vbuf[leaf], ybuf[leaf_rows(leaf), :], 0, 0)
+
+    def pair_bases():
+        ref = u1.at[upper[1]]
+        return remote(ref, ref, u_send, u_recv, partners[1])
+
+    def share_pair():
+        u1[upper[1]] = ub[1]
+        pair_bases().start()
+        ag_second(vbuf, 0)
+        leaf_part(col)
+        leaf_part(left)
+        leaf_part(right)
+
+    def wide_parts():
         def facing(t, other):
             b = coup[t]
-            low = dot_bx(b, other)
-            high = dot_bx(b, other, 0, 0)
-            return jnp.where(upper[t] == 1, high, low)
+            return jnp.where(upper[t] == 1, dot_bx(b, other, 0, 0), dot_bx(b, other))
 
         def halves(t):
             own = pl.ds(pl.multiple_of(upper[t] * R, R), R)
             other = pl.ds(pl.multiple_of((1 - upper[t]) * R, R), R)
             return ub[t + 1, own, :], ub[t + 1, other, :]
 
+        ag_last(vbuf, 0)
+        leaf_part(across)
         own1, other1 = halves(0)
         own2, other2 = halves(1)
-        v2 = dot(own1, own2)
-        c2 = -(dot(facing(0, other1), own2) + dot(own1, facing(1, other2)))
-        base = ub[0]
-        v = dot(base, v2)
-        vbuf[col] = v
-        ag_first(vbuf, 0)
-        c = dot(base, c2)
-        w = wrow[...]
-        ps[...] = dot_xb(c, w, 0, 0)
-        pp = dot_xb(v, w, 0, 0)
+        correction = -(dot(facing(0, other1), own2) + dot(own1, facing(1, other2)))
+        ref = u1.at[1 - upper[1]]
+        remote(ref, ref, u_send, u_recv, partners[1]).wait_recv()
+        down[pl.ds(0, 2 * R), :] = dot(u1[0], ub[2, LOW, :])
+        down[pl.ds(2 * R, 2 * R), :] = dot(u1[1], ub[2, HIGH, :])
+        sample = dot(down[...], s0[...], 0, 0) + dot(correction, p0[...], 0, 0)
+        proj = dot(down[pl.ds(pl.multiple_of(col * R, R), R), :], p0[...], 0, 0)
         for k in range(4):
-            sparts[k, HIGH] = pp[:, k * R : (k + 1) * R]
-
-    def relay_bases():
-        ag_second(vbuf, 0)
-
-    def wide_parts():
-        ag_last(vbuf, 0)
-
-        @pl.loop(0, 4)
-        def _(k):
-            rows = pl.ds(pl.multiple_of(k * 2 * R, R), 2 * R)
-            ps[...] += dot(vbuf[k], ybuf[rows, :], 0, 0)
-
-        for k in range(4):
-            sparts[k, LOW] = ps[:, k * R : (k + 1) * R]
+            sparts[k, LOW] = sample[:, k * R : (k + 1) * R]
+            sparts[k, HIGH] = proj[:, k * R : (k + 1) * R]
         rs_first(sparts, 1)
 
     def relay_parts():
@@ -342,6 +348,7 @@
     def wide_start():
         rs_last(sparts, 1, comm2.at[0, upper[2]])
         pair_copy(comm2, 2, 2, c2_send, c2_recv).start()
+        wide_merge(2)
 
     def wide_merge(t):
         pair_wait(comm2, 2, t, c2_send, c2_recv)
@@ -357,9 +364,8 @@
         comm2[t - 1, upper[t + 1], HIGH] = dot(u_low, low_p, 0, 0) + dot(u_high, high_p, 0, 0)
         pair_copy(comm2, 2, t + 1, c2_send, c2_recv).start()
 
-    at_start = {4: relay_parts, 5: functools.partial(wide_merge, 3)}
-    at_middle = {3: relay_bases, 4: wide_start}
-    at_end = {2: compose, 3: wide_parts, 4: functools.partial(wide_merge, 2)}
+    at_middle = {3: relay_parts}
+    at_end = {0: share_leaf, 1: share_pair, 2: wide_parts, 3: wide_start, 4: functools.partial(wide_merge, 3)}
 
     def place(table, t):
         for at, piece in table.items():
@@ -395,7 +401,6 @@
             zw[LOW, HIGH] = low_w
             zw[HIGH, HIGH] = high_w
 
-        place(at_start, t)
         z = zw[:, LOW]
         products = dot(z, zw[...], 0, 0)
         gm[...] = products
@@ -448,6 +453,7 @@
     rs_drain(zparts, 0)
     rs_drain(sparts, 1)
     ag_drain(vbuf, 0)
+    pair_bases().wait_send()
     ag_drain(topbuf, 1)
     for t in range(LEVELS):
         for i in range(pieces):
@@ -484,7 +490,8 @@
             f32(16, 8, R), f32(R, R), f32(R, 2 * R), f32(2 * R, 2 * R), f32(LEVELS + 1, 2 * R, R),
             f32(LEVELS + 1, 2, R, 2 * R), f32(3, 2, 2 * R, R), f32(2, 2, R, R), f32(2, 4, R, R), f32(2, 2, R, R),
             f32(4, 2 * R, R), f32(4, 2 * R, R), f32(4, 2 * R, R), f32(4, R, R), f32(8 * R, width), f32(R, width),
-            dma((2, 6)), dma((2, 6)), dma((2, 4)), dma((2, 4)), dma((LEVELS, 4)), dma((LEVELS, 4)), dma((3,)), dma((3,)),
+            f32(4 * R, width), f32(2, 2 * R, R), f32(4 * R, R),
+            dma((2, 6)), dma((2, 6)), dma((2, 4)), dma((2, 4)), dma((LEVELS, 4)), dma((LEVELS, 4)), dma((3,)), dma((3,)), dma, dma,
             dma((4,)), dma((6,)), dma((4,)), dma,
         ],
         compiler_params=pltpu.CompilerParams(

time: 76.3 us -> 71 us (0.931); the launches traced: 75.4 us -> 70.9 us
  Pallas kernels: 72.7 us -> 68.2 us
    pallas_call x1, Pallas kernels: 72.7 us -> 68.2 us  [run_tree(): pl.pallas_call(tree_kernel, out_shape=[jax.ShapeDtypeStruct((2 * R, R), F...]
where the time goes in v4:
time: 71 us; the launch traced here: 70.9 us
  Pallas kernels  68.2 us (96%)
  local copies, waits for them, and re-layouts  2.08 us (3%)
    pallas_call x1, Pallas kernels, run_tree(): pl.pallas_call(tree_kernel, out_shape=[jax.ShapeDtypeStruct((2 * R, R), F...  68.2 us
    unnamed x3, local copies, waits for them, and re-layouts  2.08 us

profile of v4, /device:TPU:192, one launch (start us, length us, event | category | flops | bytes accessed | tf_op | source)
XLA Modules:
  0.0 70.9 jit_solution(12584799919168777109)
XLA Ops:
  0.6 68.2 %tree.1 = (f32[256,128]{1,0:T(8,128)S(1)}, f32[5,128,128]{2,1,0:T(8,128)S(1)}, f32[128,512]{1,0:T(8,128)S(1)}) custom-call(s32[1,168]{1,0:T(1,128)} %bitcast.7, bf16[168,128,128]{2,1,0:T(8,128)(2,1)} %tiles_hbm.1, bf16[6144,512]{1,0:T(8,128)(2,1)} %sketch_hbm.1, bf16[256,512]{1,0:T(8,128)(2,1)} %wrow_hbm.1, f32[512,128]{1,0:T(8,128)} %subsk_hbm.1, ...), custom_call_target="tpu_custom_call" | custom-call | tf_op jit(solution)/shard_map/tree/pallas_call | solution.py:477
  68.8 0.7 copy.12
  69.5 0.7 %copy.13 = f32[1,5,128,128]{3,2,1,0:T(8,128)} copy(f32[1,5,128,128]{3,2,1,0:T(8,128)S(1)} %bitcast.4) | data formatting | bytes 655360
  70.2 0.7 copy.14

commit v5 on v4

--- a/solution.py
+++ b/solution.py
@@ -29,6 +29,17 @@
     rest = x - hi.astype(F32)
     mid = rest.astype(BF)
     return hi, mid, (rest - mid.astype(F32)).astype(BF)
+
+
+def split2(x):
+    hi = x.astype(BF)
+    return hi, (x - hi.astype(F32)).astype(BF)
+
+
+def dot3(a, b, ca=1, cb=0):
+    a_hi, a_lo = split2(a)
+    b_hi, b_lo = split2(b)
+    return dot16(a_hi, b_hi, ca, cb) + (dot16(a_hi, b_lo, ca, cb) + dot16(a_lo, b_hi, ca, cb))
 
 
 def dot_bx(b, x, ca=1, cb=0):
@@ -110,7 +121,7 @@
     slots_hbm, tiles_hbm, sketch_hbm, wrow_hbm, subsk_hbm, coup_hbm,
     leaf_out, trans_out, top_out,
     slots, tiles, sketch, wrow, subsk, coup, slot_pad, index_row, index,
-    work, linv, gm, zw, ub, comm, comm2, relay, fin, staged, zparts, sparts, vbuf, topbuf, ybuf, p0, s0, u1, down,
+    work, linv, gm, zw, ub, comm, comm2, relay, fin, staged, zparts, sparts, vbuf, topbuf, ybuf, p0, s0, u1, down, pq,
     rs_send, rs_recv, ag_send, ag_recv, c_send, c_recv, c2_send, c2_recv, u_send, u_recv, t_sem, k_sem, i_sem, n_sem,
 ):
     tile_count = tiles_hbm.shape[0]
@@ -216,27 +227,29 @@
     def ag_copy(buf, n, i, receive=False):
         half = buf.shape[1] // 2
         first, second = pl.ds(0, half), pl.ds(half, half)
-        if receive:
-            ref = [buf.at[left], buf.at[right], buf.at[across, first], buf.at[across, second]][i]
-        else:
-            ref = [buf.at[col], buf.at[col], buf.at[left, first], buf.at[right, second]][i]
+        part = [first, second, second, first, first, second][i]
+        source = [col, col, col, col, left, right][i]
+        target = [left, right, left, right, across, across][i]
+        ref = buf.at[target if receive else source, part]
         return remote(ref, ref, ag_send.at[n, i], ag_recv.at[n, i], [to_right, to_left][i % 2])
 
     def ag_first(buf, n):
-        for i in range(2):
+        for i in range(4):
             ag_copy(buf, n, i).start()
 
     def ag_second(buf, n):
         for i in range(2):
             ag_copy(buf, n, i, True).wait_recv()
-            ag_copy(buf, n, i + 2).start()
-
-    def ag_last(buf, n):
+            ag_copy(buf, n, i + 4).start()
         for i in range(2, 4):
             ag_copy(buf, n, i, True).wait_recv()
 
+    def ag_last(buf, n):
+        for i in range(4, 6):
+            ag_copy(buf, n, i, True).wait_recv()
+
     def ag_drain(buf, n):
-        for i in range(4):
+        for i in range(6):
             ag_copy(buf, n, i).wait_send()
 
     def pair_copy(buf, base, t, send, recv):
@@ -284,12 +297,11 @@
         copy.wait()
     load_sketch(2, k_sem.shape[0])
     small.append(load(coup_hbm, coup, i_sem.at[3]))
-    partial_samples([across], col_tiles // k_sem.shape[0], True)
-    for i in range(2):
+    partial_samples([across, right], col_tiles // k_sem.shape[0], True)
+    for i in range(3):
         rs_copy(zparts, 0, i).start()
-    partial_samples([right, left], 8, False)
-    for i in range(2, 4):
-        rs_copy(zparts, 0, i).start()
+    partial_samples([left], 16, False)
+    rs_copy(zparts, 0, 3).start()
     rs_second(zparts, 0)
     partial_samples([col], 16, False)
     small[3].wait()
@@ -302,7 +314,7 @@
 
     def leaf_part(leaf):
         rows = pl.ds(pl.multiple_of(leaf * R, R), R)
-        s0[rows, :] = dot(vbuf[leaf], ybuf[leaf_rows(leaf), :], 0, 0)
+        s0[rows, :] = dot3(vbuf[leaf], ybuf[leaf_rows(leaf), :], 0, 0)
 
     def pair_bases():
         ref = u1.at[upper[1]]
@@ -335,8 +347,8 @@
         remote(ref, ref, u_send, u_recv, partners[1]).wait_recv()
         down[pl.ds(0, 2 * R), :] = dot(u1[0], ub[2, LOW, :])
         down[pl.ds(2 * R, 2 * R), :] = dot(u1[1], ub[2, HIGH, :])
-        sample = dot(down[...], s0[...], 0, 0) + dot(correction, p0[...], 0, 0)
-        proj = dot(down[pl.ds(pl.multiple_of(col * R, R), R), :], p0[...], 0, 0)
+        sample = dot3(down[...], s0[...], 0, 0) + dot3(correction, p0[...], 0, 0)
+        proj = dot3(down[pl.ds(pl.multiple_of(col * R, R), R), :], p0[...], 0, 0)
         for k in range(4):
             sparts[k, LOW] = sample[:, k * R : (k + 1) * R]
             sparts[k, HIGH] = proj[:, k * R : (k + 1) * R]
@@ -346,22 +358,23 @@
         rs_second(sparts, 1)
 
     def wide_start():
-        rs_last(sparts, 1, comm2.at[0, upper[2]])
+        rs_last(sparts, 1, zw.at[:, LOW])
+        comm2[0, upper[2], :, LOW] = zw[LOW, LOW]
+        comm2[0, upper[2], :, HIGH] = zw[HIGH, LOW]
         pair_copy(comm2, 2, 2, c2_send, c2_recv).start()
         wide_merge(2)
 
     def wide_merge(t):
         pair_wait(comm2, 2, t, c2_send, c2_recv)
-        low_p, high_p = comm2[t - 2, 0, HIGH], comm2[t - 2, 1, HIGH]
-        low = comm2[t - 2, 0, LOW] - dot_bx(coup[t], high_p)
-        high = comm2[t - 2, 1, LOW] - dot_bx(coup[t], low_p, 0, 0)
-        u_low, u_high = ub[t + 1, LOW, :], ub[t + 1, HIGH, :]
-        sample = dot(u_low, low, 0, 0) + dot(u_high, high, 0, 0)
+        low_p, high_p = comm2[t - 2, 0, :, HIGH], comm2[t - 2, 1, :, HIGH]
+        pq[LOW, LOW] = comm2[t - 2, 0, :, LOW] - dot_bx(coup[t], high_p)
+        pq[HIGH, LOW] = comm2[t - 2, 1, :, LOW] - dot_bx(coup[t], low_p, 0, 0)
         if t == LEVELS - 1:
-            topbuf[col] = sample
+            topbuf[col] = dot3(ub[t + 1], pq[:, LOW], 0, 0)
             return
-        comm2[t - 1, upper[t + 1], LOW] = sample
-        comm2[t - 1, upper[t + 1], HIGH] = dot(u_low, low_p, 0, 0) + dot(u_high, high_p, 0, 0)
+        pq[LOW, HIGH] = low_p
+        pq[HIGH, HIGH] = high_p
+        comm2[t - 1, upper[t + 1]] = dot3(ub[t + 1], pq[...], 0, 0)
         pair_copy(comm2, 2, t + 1, c2_send, c2_recv).start()
 
     at_middle = {3: relay_parts}
@@ -488,10 +501,10 @@
             f32(width, R), pltpu.VMEM(couplings.shape, BF), pltpu.VMEM((1, 2 * R), jnp.int32),
             pltpu.VMEM((1, slot_count), jnp.int32), pltpu.SMEM((1, slot_count), jnp.int32),
             f32(16, 8, R), f32(R, R), f32(R, 2 * R), f32(2 * R, 2 * R), f32(LEVELS + 1, 2 * R, R),
-            f32(LEVELS + 1, 2, R, 2 * R), f32(3, 2, 2 * R, R), f32(2, 2, R, R), f32(2, 4, R, R), f32(2, 2, R, R),
+            f32(LEVELS + 1, 2, R, 2 * R), f32(3, 2, R, 2 * R), f32(2, 2, R, R), f32(2, 4, R, R), f32(2, 2, R, R),
             f32(4, 2 * R, R), f32(4, 2 * R, R), f32(4, 2 * R, R), f32(4, R, R), f32(8 * R, width), f32(R, width),
-            f32(4 * R, width), f32(2, 2 * R, R), f32(4 * R, R),
-            dma((2, 6)), dma((2, 6)), dma((2, 4)), dma((2, 4)), dma((LEVELS, 4)), dma((LEVELS, 4)), dma((3,)), dma((3,)), dma, dma,
+            f32(4 * R, width), f32(2, 2 * R, R), f32(4 * R, R), f32(2 * R, 2 * R),
+            dma((2, 6)), dma((2, 6)), dma((2, 6)), dma((2, 6)), dma((LEVELS, 4)), dma((LEVELS, 4)), dma((3,)), dma((3,)), dma, dma,
             dma((4,)), dma((6,)), dma((4,)), dma,
         ],
         compiler_params=pltpu.CompilerParams(
@@ -501,10 +514,33 @@
     )(*[pltpu.with_memory_space_constraint(a, pltpu.HBM) for a in (slots, tiles, sketch, wrow, subsketch, couplings)])
 
 
+def store_kernel(*refs):
+    copies = [pltpu.make_async_copy(refs[i], refs[i + 3], refs[6].at[i]) for i in range(3)]
+    for copy in copies:
+        copy.start()
+    for copy in copies:
+        copy.wait()
+
+
+def store(*results):
+    vmem = pl.BlockSpec(memory_space=pltpu.VMEM)
+    hbm = pl.BlockSpec(memory_space=pl.ANY)
+    return pl.pallas_call(
+        store_kernel,
+        out_shape=[jax.ShapeDtypeStruct(a.shape, a.dtype) for a in results],
+        in_specs=[vmem] * 3,
+        out_specs=[hbm] * 3,
+        scratch_shapes=[pltpu.SemaphoreType.DMA((3,))],
+        compiler_params=pltpu.CompilerParams(vmem_limit_bytes=2**20),
+        name="store",
+    )(*results)
+
+
 def per_device(tiles, tile_slots, sketch, row_sketch, subsketch, couplings):
     leaf_basis, transfer, top = run_tree(
         tile_slots.reshape(1, -1), tiles, sketch, row_sketch, subsketch, couplings[0]
     )
+    leaf_basis, transfer, top = store(leaf_basis, transfer, top)
     return leaf_basis, transfer[None], top[None]
 
 

time: 71 us -> 68.1 us (0.959)
  local copies, waits for them, and re-layouts: 2.08 us -> 0 us
  Pallas kernels: 68.2 us -> 67.3 us
    unnamed x3 -> x0, local copies, waits for them, and re-layouts: 2.08 us -> none
    pallas_call x1, Pallas kernels: 68.2 us -> 66.5 us  [run_tree(): pl.pallas_call(tree_kernel, out_shape=[jax.ShapeDtypeStruct((2 * R, R), F...]
    pallas_call x0 -> x1, Pallas kernels: none -> 0.88 us  [store(): pl.pallas_call(store_kernel, out_shape=[jax.ShapeDtypeStruct(a.shape, a.d...]
where the time goes in v5:
time: 68.1 us; the launch traced here: 68 us
  Pallas kernels  67.3 us (99%)
    pallas_call x1, Pallas kernels, run_tree(): pl.pallas_call(tree_kernel, out_shape=[jax.ShapeDtypeStruct((2 * R, R), F...  66.5 us

profile of v5, /device:TPU:192, one launch (start us, length us, event | category | flops | bytes accessed | tf_op | source)
XLA Modules:
  0.0 68.0 jit_solution(16469220892471330897)
XLA Ops:
  0.6 66.5 %tree.1 = (f32[256,128]{1,0:T(8,128)S(1)}, f32[5,128,128]{2,1,0:T(8,128)S(1)}, f32[128,512]{1,0:T(8,128)S(1)}) custom-call(s32[1,168]{1,0:T(1,128)} %bitcast.5, bf16[168,128,128]{2,1,0:T(8,128)(2,1)} %tiles_hbm.1, bf16[6144,512]{1,0:T(8,128)(2,1)} %sketch_hbm.1, bf16[256,512]{1,0:T(8,128)(2,1)} %wrow_hbm.1, f32[512,128]{1,0:T(8,128)} %subsk_hbm.1, ...), custom_call_target="tpu_custom_call" | custom-call | tf_op jit(solution)/shard_map/tree/pallas_call | solution.py:490
  67.1 0.9 %store.1 = (f32[256,128]{1,0:T(8,128)}, f32[5,128,128]{2,1,0:T(8,128)}, f32[128,512]{1,0:T(8,128)}) custom-call(f32[256,128]{1,0:T(8,128)S(1)} %get-tuple-element.9.refs_0_, f32[5,128,128]{2,1,0:T(8,128)S(1)} %get-tuple-element.10.refs_1_, f32[128,512]{1,0:T(8,128)S(1)} %get-tuple-element.11.refs_2_), custom_call_target="tpu_custom_call" | custom-call | tf_op jit(solution)/shard_map/store/pallas_call | solution.py:528

commit v6 on v5

--- a/solution.py
+++ b/solution.py
@@ -40,6 +40,13 @@
     a_hi, a_lo = split2(a)
     b_hi, b_lo = split2(b)
     return dot16(a_hi, b_hi, ca, cb) + (dot16(a_hi, b_lo, ca, cb) + dot16(a_lo, b_hi, ca, cb))
+
+
+def dot6(a, b, ca=1, cb=0):
+    a0, a1, a2 = split3(a)
+    b0, b1, b2 = split3(b)
+    small = dot16(a0, b2, ca, cb) + (dot16(a1, b1, ca, cb) + dot16(a2, b0, ca, cb))
+    return dot16(a0, b0, ca, cb) + (dot16(a0, b1, ca, cb) + (dot16(a1, b0, ca, cb) + small))
 
 
 def dot_bx(b, x, ca=1, cb=0):
@@ -287,7 +294,7 @@
                 ybuf[leaf_rows(leaf), :] += product[i * 2 * R : (i + 1) * 2 * R]
 
         for leaf in leaves:
-            zparts[leaf] = dot(ybuf[leaf_rows(leaf), :], subsk[...])
+            zparts[leaf] = dot6(ybuf[leaf_rows(leaf), :], subsk[...])
 
     small[1].wait()
     small[2].wait()
@@ -342,11 +349,11 @@
         leaf_part(across)
         own1, other1 = halves(0)
         own2, other2 = halves(1)
-        correction = -(dot(facing(0, other1), own2) + dot(own1, facing(1, other2)))
+        correction = -(dot(facing(0, other1), own2) + dot6(own1, facing(1, other2)))
         ref = u1.at[1 - upper[1]]
         remote(ref, ref, u_send, u_recv, partners[1]).wait_recv()
-        down[pl.ds(0, 2 * R), :] = dot(u1[0], ub[2, LOW, :])
-        down[pl.ds(2 * R, 2 * R), :] = dot(u1[1], ub[2, HIGH, :])
+        down[pl.ds(0, 2 * R), :] = dot6(u1[0], ub[2, LOW, :])
+        down[pl.ds(2 * R, 2 * R), :] = dot6(u1[1], ub[2, HIGH, :])
         sample = dot3(down[...], s0[...], 0, 0) + dot3(correction, p0[...], 0, 0)
         proj = dot3(down[pl.ds(pl.multiple_of(col * R, R), R), :], p0[...], 0, 0)
         for k in range(4):
@@ -362,7 +369,6 @@
         comm2[0, upper[2], :, LOW] = zw[LOW, LOW]
         comm2[0, upper[2], :, HIGH] = zw[HIGH, LOW]
         pair_copy(comm2, 2, 2, c2_send, c2_recv).start()
-        wide_merge(2)
 
     def wide_merge(t):
         pair_wait(comm2, 2, t, c2_send, c2_recv)
@@ -377,6 +383,7 @@
         comm2[t - 1, upper[t + 1]] = dot3(ub[t + 1], pq[...], 0, 0)
         pair_copy(comm2, 2, t + 1, c2_send, c2_recv).start()
 
+    at_start = {4: functools.partial(wide_merge, 2)}
     at_middle = {3: relay_parts}
     at_end = {0: share_leaf, 1: share_pair, 2: wide_parts, 3: wide_start, 4: functools.partial(wide_merge, 3)}
 
@@ -414,15 +421,16 @@
             zw[LOW, HIGH] = low_w
             zw[HIGH, HIGH] = high_w
 
+        place(at_start, t)
         z = zw[:, LOW]
-        products = dot(z, zw[...], 0, 0)
+        products = dot6(z, zw[...], 0, 0)
         gm[...] = products
         shift = 0.0001 * jnp.sum(z * z, keepdims=True) / R + 1e-06
         work[...] = products[:, :R].reshape(16, 8, R) + jnp.where(eye, shift.reshape(1, 1, 1), 0.0)
 
         def make_piece(i):
             rows = pl.ds(i * piece, piece)
-            comm[t, own, rows, :] = dot(linv[rows, :], gm[...])
+            comm[t, own, rows, :] = dot6(linv[rows, :], gm[...])
 
         def send_piece(i):
             @pl.when(t < LEVELS)
@@ -440,7 +448,7 @@
         factor(work, linv, one, segment)
         make_piece(pieces - 1)
         send_piece(pieces - 1)
-        u = dot(zw[:, LOW], linv[...], 1, 1)
+        u = dot6(zw[:, LOW], linv[...], 1, 1)
         ub[t] = u
 
         @pl.when(t == 0)

time: 68.1 us -> 67.1 us (0.985)
  Pallas kernels: 67.3 us -> 66.4 us
    pallas_call x1, Pallas kernels: 66.5 us -> 65.5 us  [run_tree(): pl.pallas_call(tree_kernel, out_shape=[jax.ShapeDtypeStruct((2 * R, R), F...]
where the time goes in v6:
time: 67.1 us; the launch traced here: 67 us
  Pallas kernels  66.4 us (99%)
    pallas_call x1, Pallas kernels, run_tree(): pl.pallas_call(tree_kernel, out_shape=[jax.ShapeDtypeStruct((2 * R, R), F...  65.5 us

profile of v6, /device:TPU:192, one launch (start us, length us, event | category | flops | bytes accessed | tf_op | source)
XLA Modules:
  0.0 67.0 jit_solution(8477237091024525558)
XLA Ops:
  0.6 65.5 %tree.1 = (f32[256,128]{1,0:T(8,128)S(1)}, f32[5,128,128]{2,1,0:T(8,128)S(1)}, f32[128,512]{1,0:T(8,128)S(1)}) custom-call(s32[1,168]{1,0:T(1,128)} %bitcast.5, bf16[168,128,128]{2,1,0:T(8,128)(2,1)} %tiles_hbm.1, bf16[6144,512]{1,0:T(8,128)(2,1)} %sketch_hbm.1, bf16[256,512]{1,0:T(8,128)(2,1)} %wrow_hbm.1, f32[512,128]{1,0:T(8,128)} %subsk_hbm.1, ...), custom_call_target="tpu_custom_call" | custom-call | tf_op jit(solution)/shard_map/tree/pallas_call | solution.py:498
  66.2 0.9 %store.1 = (f32[256,128]{1,0:T(8,128)}, f32[5,128,128]{2,1,0:T(8,128)}, f32[128,512]{1,0:T(8,128)}) custom-call(f32[256,128]{1,0:T(8,128)S(1)} %get-tuple-element.9.refs_0_, f32[5,128,128]{2,1,0:T(8,128)S(1)} %get-tuple-element.10.refs_1_, f32[128,512]{1,0:T(8,128)S(1)} %get-tuple-element.11.refs_2_), custom_call_target="tpu_custom_call" | custom-call | tf_op jit(solution)/shard_map/store/pallas_call | solution.py:536

commit v7 on v6

--- a/solution.py
+++ b/solution.py
@@ -280,18 +280,21 @@
         )
 
     def partial_samples(leaves, count, arriving):
-        for leaf in leaves:
-            ybuf[leaf_rows(leaf), :] = jnp.zeros((2 * R, ybuf.shape[1]), F32)
-
-        @pl.loop(0, col_tiles // count)
-        def _(p):
-            rows = pl.ds(pl.multiple_of(p * count * R, R), count * R)
+        def step(start, p, first):
+            rows = pl.ds(start, count * R)
             if arriving:
                 pltpu.make_async_copy(sketch_hbm.at[rows], sketch.at[rows], k_sem.at[p]).wait()
             lhs = jnp.concatenate([block_rows(leaf, p * count, count) for leaf in leaves], axis=0)
             product = dot16(lhs, sketch[rows, :])
             for i, leaf in enumerate(leaves):
-                ybuf[leaf_rows(leaf), :] += product[i * 2 * R : (i + 1) * 2 * R]
+                part = product[i * 2 * R : (i + 1) * 2 * R]
+                ybuf[leaf_rows(leaf), :] = part if first else ybuf[leaf_rows(leaf), :] + part
+
+        step(0, 0, True)
+
+        @pl.loop(1, col_tiles // count)
+        def _(p):
+            step(pl.multiple_of(p * count * R, R), p, False)
 
         for leaf in leaves:
             zparts[leaf] = dot6(ybuf[leaf_rows(leaf), :], subsk[...])

time: 67.1 us -> 67.1 us (level)
  no operation moved by 1% of the time
where the time goes in v7:
time: 67.1 us; the launch traced here: 67 us
  Pallas kernels  66.4 us (99%)
    pallas_call x1, Pallas kernels, run_tree(): pl.pallas_call(tree_kernel, out_shape=[jax.ShapeDtypeStruct((2 * R, R), F...  65.5 us

profile of v7, /device:TPU:192, one launch (start us, length us, event | category | flops | bytes accessed | tf_op | source)
XLA Modules:
  0.0 67.0 jit_solution(3110948145520478743)
XLA Ops:
  0.6 65.5 %tree.1 = (f32[256,128]{1,0:T(8,128)S(1)}, f32[5,128,128]{2,1,0:T(8,128)S(1)}, f32[128,512]{1,0:T(8,128)S(1)}) custom-call(s32[1,168]{1,0:T(1,128)} %bitcast.5, bf16[168,128,128]{2,1,0:T(8,128)(2,1)} %tiles_hbm.1, bf16[6144,512]{1,0:T(8,128)(2,1)} %sketch_hbm.1, bf16[256,512]{1,0:T(8,128)(2,1)} %wrow_hbm.1, f32[512,128]{1,0:T(8,128)} %subsk_hbm.1, ...), custom_call_target="tpu_custom_call" | custom-call | tf_op jit(solution)/shard_map/tree/pallas_call | solution.py:501
  66.1 0.9 %store.1 = (f32[256,128]{1,0:T(8,128)}, f32[5,128,128]{2,1,0:T(8,128)}, f32[128,512]{1,0:T(8,128)}) custom-call(f32[256,128]{1,0:T(8,128)S(1)} %get-tuple-element.9.refs_0_, f32[5,128,128]{2,1,0:T(8,128)S(1)} %get-tuple-element.10.refs_1_, f32[128,512]{1,0:T(8,128)S(1)} %get-tuple-element.11.refs_2_), custom_call_target="tpu_custom_call" | custom-call | tf_op jit(solution)/shard_map/store/pallas_call | solution.py:539
